TPU v7x, 32 devices: a whole 2x2x4 slice. The times are simulated.
32 devices in a mesh: expert: 8 (over z, x), dp: 4 (over y, core).
Axes of the slice: x: 2, y: 2, z: 4, core: 2. Of those that a mesh axis runs over, the one named last changes fastest.
Arguments:
- tokens: bfloat16 [8192, 1024], P(('expert', 'dp')), may hold values from -6 to 6
- route_ids: int32 [8192, 2], P(('expert', 'dp')), may hold values from 0 to 7, all different within a row; in each aligned block of 256 rows (0 to 255, 256 to 511, ...) at most 96 rows name the same one
- gate_values: float32 [8192, 2], P(('expert', 'dp')), may hold values from 0.2 to 1
- w_gate: bfloat16 [8, 1024, 1024], P('expert', 'dp'), may hold values from -0.1875 to 0.1875
- w_up: bfloat16 [8, 1024, 1024], P('expert', 'dp'), may hold values from -0.1875 to 0.1875
- w_down: bfloat16 [8, 1024, 1024], P('expert', 'dp'), may hold values from -0.1875 to 0.1875
- swap_flags: int32 [8], replicated, may hold values from 0 to 1, as said below
- out_grad: bfloat16 [8192, 1024], P(('expert', 'dp')), may hold values from -6 to 6
Outputs:
- layer_out: bfloat16 [8192, 1024], P(('expert', 'dp'))
- grad_tokens: bfloat16 [8192, 1024], P(('expert', 'dp'))
- grad_gate: float32 [8, 1024, 1024], P('expert', 'dp')
- grad_up: float32 [8, 1024, 1024], P('expert', 'dp')
- grad_down: float32 [8, 1024, 1024], P('expert', 'dp')
Inputs may be any that keep to these rules, and one draw needn't show every extreme that they name: `route_ids`: within the rows of one device (256 tokens) no expert is named by more than 96 token-expert pairs, a bound that some block reaches; a token's 2 experts differ. `swap_flags`: the first and the last pair always exchange their experts.
All inputs are finite; a program needn't handle non-finite values.
Results may differ from a plain program's by a relative error of at most 0.012.
Values may be sent and summed in bfloat16 or wider, within the bound.
A program may use at most 64 MiB of HBM per device.

v0:
```python
import jax
import jax.numpy as jnp
from jax import lax
from jax.sharding import PartitionSpec as P


def swapped(shard, axis, stride):
    return lax.ppermute(shard, axis, [(i, i ^ 1 << stride) for i in range(lax.axis_size(axis))])


def pair_moves(swap_flags, index_of, half_axis):
    pair_of = index_of % half_axis
    return jnp.take(swap_flags, pair_of) != jnp.take(swap_flags, pair_of + half_axis)


def route_slots(route_ids, exp_dev, axis_len, slot_cap):
    chosen = route_ids.reshape(-1)
    holder = chosen // exp_dev
    match_table = (
        chosen[:, None] == jnp.arange(exp_dev * axis_len, dtype=jnp.int32)[None, :]
    ).astype(jnp.int32)
    rank_of = jnp.sum(jnp.cumsum(match_table, axis=0) * match_table, axis=1) - 1
    return (holder * exp_dev + chosen % exp_dev) * slot_cap + rank_of


def shards(tokens, route_ids, gate_values, w_gate, w_up, w_down, swap_flags, out_grad):
    axis_len = lax.axis_size("expert")
    own_index = lax.axis_index("expert")
    half_axis = axis_len // 2
    swap_bit = axis_len.bit_length() - 2
    exp_dev = w_gate.shape[0]
    tok_rows = tokens.shape[0]
    feature_count = tokens.shape[1]
    top_k = route_ids.shape[1]
    copies = tok_rows * top_k
    slot_cap = 3 * copies // (2 * exp_dev * axis_len)
    paired_here = pair_moves(swap_flags, own_index, half_axis)
    slot_index = route_slots(route_ids, exp_dev, axis_len, slot_cap)
    total_slots = axis_len * exp_dev * slot_cap
    source = (
        jnp.full((total_slots,), copies, jnp.int32)
        .at[slot_index]
        .set(jnp.arange(copies, dtype=jnp.int32))
    )
    filled = (source < copies)[:, None]
    picked = jnp.minimum(source, copies - 1)
    weights_flat = gate_values.reshape(-1)
    buffer_shape = (axis_len, exp_dev, slot_cap, feature_count)
    send_x = jnp.where(filled, tokens[picked // top_k], jnp.zeros((), jnp.bfloat16)).reshape(
        buffer_shape
    )
    cot_rows = (
        weights_flat[picked][:, None] * out_grad[picked // top_k].astype(jnp.float32)
    ).astype(jnp.bfloat16)
    send_c = jnp.where(filled, cot_rows, jnp.zeros((), jnp.bfloat16)).reshape(buffer_shape)
    recv_x = lax.all_to_all(send_x, "expert", split_axis=0, concat_axis=0, tiled=True)
    full_gate, full_up, full_down = (
        lax.all_gather(w_gate, "dp", axis=1, tiled=True),
        lax.all_gather(w_up, "dp", axis=1, tiled=True),
        lax.all_gather(w_down, "dp", axis=1, tiled=True),
    )
    pre_gate = jnp.einsum("secd,edf->secf", recv_x, full_gate, preferred_element_type=jnp.float32)
    pre_up = jnp.einsum("secd,edf->secf", recv_x, full_up, preferred_element_type=jnp.float32)
    hidden = (jax.nn.silu(pre_gate) * pre_up).astype(jnp.bfloat16)
    expert_out = jnp.einsum(
        "secf,efd->secd", hidden, full_down, preferred_element_type=jnp.float32
    ).astype(jnp.bfloat16)
    returned_out = lax.all_to_all(
        expert_out, "expert", split_axis=0, concat_axis=0, tiled=True
    ).reshape(total_slots, feature_count)
    weighted = returned_out[slot_index].astype(jnp.float32) * weights_flat[:, None]
    layer_out = jnp.sum(weighted.reshape(tok_rows, top_k, feature_count), axis=1).astype(
        jnp.bfloat16
    )
    recv_c = lax.all_to_all(send_c, "expert", split_axis=0, concat_axis=0, tiled=True)
    grad_h = jnp.einsum("secd,efd->secf", recv_c, full_down, preferred_element_type=jnp.float32)
    sigmoid_a = jax.nn.sigmoid(pre_gate)
    grad_a = (grad_h * pre_up * sigmoid_a * (1.0 + pre_gate * (1.0 - sigmoid_a))).astype(
        jnp.bfloat16
    )
    grad_b = (grad_h * pre_gate * sigmoid_a).astype(jnp.bfloat16)
    copy_sum = jnp.einsum("secf,edf->secd", grad_a, full_gate, preferred_element_type=jnp.float32)
    copy_sum = copy_sum + jnp.einsum(
        "secf,edf->secd", grad_b, full_up, preferred_element_type=jnp.float32
    )
    copy_grad = copy_sum.astype(jnp.bfloat16)
    returned_grad = lax.all_to_all(
        copy_grad, "expert", split_axis=0, concat_axis=0, tiled=True
    ).reshape(total_slots, feature_count)
    grad_tokens = jnp.sum(
        returned_grad[slot_index].astype(jnp.float32).reshape(tok_rows, top_k, feature_count),
        axis=1,
    ).astype(jnp.bfloat16)
    dw_gate = jnp.einsum("secd,secf->edf", recv_x, grad_a, preferred_element_type=jnp.float32)
    dw_up = jnp.einsum("secd,secf->edf", recv_x, grad_b, preferred_element_type=jnp.float32)
    dw_down = jnp.einsum("secf,secd->efd", hidden, recv_c, preferred_element_type=jnp.float32)
    summed = (
        lax.psum_scatter(
            dw_gate.astype(jnp.bfloat16), "dp", scatter_dimension=1, tiled=True
        ).astype(jnp.float32),
        lax.psum_scatter(dw_up.astype(jnp.bfloat16), "dp", scatter_dimension=1, tiled=True).astype(
            jnp.float32
        ),
        lax.psum_scatter(
            dw_down.astype(jnp.bfloat16), "dp", scatter_dimension=1, tiled=True
        ).astype(jnp.float32),
    )
    swapped_grads = (
        swapped(summed[0].astype(jnp.bfloat16), "expert", swap_bit).astype(jnp.float32),
        swapped(summed[1].astype(jnp.bfloat16), "expert", swap_bit).astype(jnp.float32),
        swapped(summed[2].astype(jnp.bfloat16), "expert", swap_bit).astype(jnp.float32),
    )
    summed = (
        jnp.where(paired_here, swapped_grads[0], summed[0]),
        jnp.where(paired_here, swapped_grads[1], summed[1]),
        jnp.where(paired_here, swapped_grads[2], summed[2]),
    )
    return (layer_out, grad_tokens, summed[0], summed[1], summed[2])


def solution(mesh):
    in_specs = (
        P(("expert", "dp"), None),
        P(("expert", "dp"), None),
        P(("expert", "dp"), None),
        P("expert", "dp", None),
        P("expert", "dp", None),
        P("expert", "dp", None),
        P(),
        P(("expert", "dp"), None),
    )
    out_specs = (
        P(("expert", "dp"), None),
        P(("expert", "dp"), None),
        P("expert", "dp", None),
        P("expert", "dp", None),
        P("expert", "dp", None),
    )
    return jax.shard_map(shards, mesh=mesh, in_specs=in_specs, out_specs=out_specs, check_vma=False)
```

profile of v0, /device:TPU:31, one launch (start us, length us, event | category | flops | bytes accessed | tf_op | source)
XLA Modules:
  0.0 299.6 jit_solution(6092971207498117455)
XLA Ops:
  7.2 0.0 copy-start
  7.2 0.0 all-gather.4.cloned.1.call-start
  7.2 0.7 all-gather.4.cloned.1.call-update
  7.9 0.0 all-gather.6.cloned.1.call-start
  8.0 0.7 all-gather.6.cloned.1.call-update
  8.7 0.8 copy.20
  9.5 0.1 eq.33
  9.6 0.1 eq.29
  9.8 0.7 broadcast_multiply_fusion
  10.5 1.1 reduce-window.6
  11.6 0.2 slice_reduce_fusion
  11.9 0.1 fusion.52
  11.9 0.1 copy.19
  12.1 0.1 mul.72
  12.3 2.4 scatter_custom_fusion
  14.8 0.0 copy-start.1
  14.8 2.8 gather_fusion
  17.6 0.0 copy-start.6
  17.6 3.6 %gather_fusion.3 = bf16[768,1024]{1,0:T(8,128)(2,1)} fusion(bf16[256,1024]{1,0:T(8,128)(2,1)S(1)} %copy-done.1, s32[1024]{0:T(1024)S(1)} %get-tuple-element.37), kind=kCustom, calls=%fused_computation.3 | custom fusion | bytes 3148800 | tf_op jit(solution)/shard_map/gather | solution.py:53
  21.2 0.1 copy.24
  21.3 0.1 reshape.197
  21.5 5.0 %gather_fusion.2 = f32[768]{0:T(1024)S(1)} fusion(f32[512]{0:T(512)S(1)} %reshape.197, s32[1024]{0:T(1024)S(1)} %get-tuple-element.36), kind=kCustom, calls=%fused_computation.2 | custom fusion | bytes 9216 | tf_op jit(solution)/shard_map/gather | solution.py:53
  26.5 0.1 mul.78
  26.6 0.1 broadcast_in_dim.38
  26.7 3.8 %fusion.30 = (bf16[8,1,96,1024]{3,2,1,0:T(8,128)(2,1)}, bf16[8,1,96,1024]{3,2,1,0:T(8,128)(2,1)}) fusion(bf16[8,1,96,1024]{3,2,1,0:T(8,128)(2,1)} %bitcast.171, f32[8,96]{1,0:T(8,128)S(1)} %mul.78, pred[8,96]{1,0:T(8,128)(4,1)S(1)} %broadcast_in_dim.38, bf16[8,1,96,1024]{3,2,1,0:T(8,128)(2,1)S(1)} %bitcast.170), kind=kLoop, calls=%fused_computation.46 | loop fusion | flops 3932160 | bytes 6295296 | tf_op jit(solution)/shard_map/jit(_where)/select_n | solution.py:55
  30.5 5.4 %all-to-all-start = ((bf16[8,1,96,1024]{3,2,1,0:T(8,128)(2,1)}), bf16[8,1,96,1024]{3,2,1,0:T(8,128)(2,1)S(1)}, u32[]{:S(2)}, u32[]{:S(2)}) async-start(bf16[8,1,96,1024]{3,2,1,0:T(8,128)(2,1)} %get-tuple-element.33), calls=%async_computation | async-start | bytes 3145728 | tf_op jit(solution)/shard_map/all_to_all | solution.py:56
  35.9 0.7 all-gather.8.cloned.1.call-update
  36.6 34.7 %all-to-all-done = bf16[8,1,96,1024]{3,2,1,0:T(8,128)(2,1)S(1)} async-done(((bf16[8,1,96,1024]{3,2,1,0:T(8,128)(2,1)}), bf16[8,1,96,1024]{3,2,1,0:T(8,128)(2,1)S(1)}, u32[]{:S(2)}, u32[]{:S(2)}) %all-to-all-start) | async-done | bytes 1572896 | tf_op jit(solution)/shard_map/all_to_all | solution.py:56
  71.3 5.4 %all-to-all-start.2 = ((bf16[8,1,96,1024]{3,2,1,0:T(8,128)(2,1)}), bf16[8,1,96,1024]{3,2,1,0:T(8,128)(2,1)}, u32[]{:S(2)}, u32[]{:S(2)}) async-start(bf16[8,1,96,1024]{3,2,1,0:T(8,128)(2,1)} %get-tuple-element.32), calls=%async_computation.2 | async-start | bytes 3145728 | tf_op jit(solution)/shard_map/all_to_all | solution.py:75
  76.7 0.0 reduce-scatter.8.cloned.1.call-start
  76.7 5.1 %fusion.21 = f32[8,96,1024]{2,1,0:T(8,128)} fusion(bf16[1,1024,1024]{2,1,0:T(8,128)(2,1)} %all-gather.4.cloned.1.call-done, bf16[8,1,96,1024]{3,2,1,0:T(8,128)(2,1)S(1)} %all-to-all-done), kind=kOutput, calls=%fused_computation.38 | convolution fusion | flops 1610612736 | bytes 6815744 | tf_op jit(solution)/shard_map/secd,edf->secf/dot_general | solution.py:62
  81.8 5.0 %fusion.17 = f32[8,96,1024]{2,1,0:T(8,128)} fusion(bf16[1,1024,1024]{2,1,0:T(8,128)(2,1)} %all-gather.6.cloned.1.call-done, bf16[8,1,96,1024]{3,2,1,0:T(8,128)(2,1)S(1)} %all-to-all-done), kind=kOutput, calls=%fused_computation.34 | convolution fusion | flops 1610612736 | bytes 6815744 | tf_op jit(solution)/shard_map/secd,edf->secf/dot_general | solution.py:63
  86.8 25.4 %all-to-all-done.2 = bf16[8,1,96,1024]{3,2,1,0:T(8,128)(2,1)} async-done(((bf16[8,1,96,1024]{3,2,1,0:T(8,128)(2,1)}), bf16[8,1,96,1024]{3,2,1,0:T(8,128)(2,1)}, u32[]{:S(2)}, u32[]{:S(2)}) %all-to-all-start.2) | async-done | bytes 1572896 | tf_op jit(solution)/shard_map/all_to_all | solution.py:75
  112.2 8.4 %fusion.3 = (bf16[8,1,96,1024]{3,2,0,1:T(8,128)(2,1)}, bf16[8,1,96,1024]{3,2,0,1:T(8,128)(2,1)S(1)}, bf16[8,1,96,1024]{3,2,0,1:T(8,128)(2,1)}) fusion(f32[8,96,1024]{2,1,0:T(8,128)} %fusion.17, f32[8,96,1024]{2,1,0:T(8,128)} %fusion.21, bf16[1,1024,1024]{2,1,0:T(8,128)(2,1)} %all-gather.8.cloned.1.call-done, bf16[8,1,96,1024]{3,2,1,0:T(8,128)(2,1)} %all-to-all-done.2), kind=kOutput, calls=%fused_computation.15 | convolution fusion | flops 1623195648 | bytes 14680064 | tf_op jit(solution)/shard_map/secd,efd->secf/dot_general | solution.py:76
  120.7 1.2 copy-done.11
  121.8 4.6 %fusion.28 = bf16[1,1024,1024]{2,1,0:T(8,128)(2,1)} fusion(bf16[8,1,96,1024]{3,2,1,0:T(8,128)(2,1)} %all-to-all-done.2, bf16[8,1,96,1024]{3,2,0,1:T(8,128)(2,1)S(1)} %get-tuple-element.28), kind=kOutput, calls=%fused_computation.44 | convolution fusion | flops 1611661312 | bytes 5242880 | tf_op jit(solution)/shard_map/secf,secd->efd/dot_general | solution.py:96
  126.4 0.0 reduce-scatter.8.cloned.1.call-update
  126.4 0.0 reduce-scatter.6.cloned.1.call-start
  126.5 4.6 %fusion.27 = bf16[1,1024,1024]{2,1,0:T(8,128)(2,1)} fusion(bf16[8,1,96,1024]{3,2,0,1:T(8,128)(2,1)} %get-tuple-element.29, bf16[8,1,96,1024]{3,2,1,0:T(8,128)(2,1)S(1)} %all-to-all-done), kind=kOutput, calls=%fused_computation.43 | convolution fusion | flops 1611661312 | bytes 5242880 | tf_op jit(solution)/shard_map/secd,secf->edf/dot_general | solution.py:95
  131.1 0.0 reduce-scatter.6.cloned.1.call-update
  131.1 1.6 copy-done.9
  132.7 3.5 %fusion.15 = f32[8,96,1024]{2,1,0:T(8,128)S(1)} fusion(bf16[1,1024,1024]{2,1,0:T(8,128)(2,1)S(1)} %copy-done.9, bf16[8,1,96,1024]{3,2,0,1:T(8,128)(2,1)} %get-tuple-element.29), kind=kOutput, calls=%fused_computation.32 | convolution fusion | flops 1610612736 | bytes 6815744 | tf_op jit(solution)/shard_map/secf,edf->secd/dot_general | solution.py:83
  136.2 3.0 %fusion.29 = bf16[8,1,96,1024]{3,2,1,0:T(8,128)(2,1)} fusion(f32[8,96,1024]{2,1,0:T(8,128)S(1)} %fusion.15, bf16[1,1024,1024]{2,1,0:T(8,128)(2,1)S(1)} %copy-done.8, bf16[8,1,96,1024]{3,2,0,1:T(8,128)(2,1)S(1)} %copy-done.10), kind=kOutput, calls=%fused_computation.45 | convolution fusion | flops 1612185600 | bytes 8388608 | tf_op jit(solution)/shard_map/secf,edf->secd/dot_general | solution.py:82
  139.2 5.4 %all-to-all-start.3 = ((bf16[8,1,96,1024]{3,2,1,0:T(8,128)(2,1)}), bf16[8,1,96,1024]{3,2,1,0:T(8,128)(2,1)S(1)}, u32[]{:S(2)}, u32[]{:S(2)}) async-start(bf16[8,1,96,1024]{3,2,1,0:T(8,128)(2,1)} %fusion.29), calls=%async_computation.3 | async-start | bytes 3145728 | tf_op jit(solution)/shard_map/all_to_all | solution.py:87
  144.6 5.1 %fusion.26 = bf16[1,1024,1024]{2,1,0:T(8,128)(2,1)} fusion(bf16[8,1,96,1024]{3,2,0,1:T(8,128)(2,1)} %get-tuple-element.27, bf16[8,1,96,1024]{3,2,1,0:T(8,128)(2,1)} %copy-done.2), kind=kOutput, calls=%fused_computation.42 | convolution fusion | flops 1611661312 | bytes 5242880 | tf_op jit(solution)/shard_map/secd,secf->edf/dot_general | solution.py:94
  149.7 0.0 reduce-scatter.4.cloned.1.call-update
  149.7 5.1 %fusion.47 = bf16[8,1,96,1024]{3,2,1,0:T(8,128)(2,1)} fusion(bf16[1,1024,1024]{2,1,0:T(8,128)(2,1)} %all-gather.8.cloned.1.call-done, bf16[8,1,96,1024]{3,2,0,1:T(8,128)(2,1)} %copy-done.11), kind=kOutput, calls=%fused_computation.60 | convolution fusion | flops 1611399168 | bytes 5242880 | tf_op jit(solution)/shard_map/secf,efd->secd/dot_general | solution.py:65
  154.8 25.2 %all-to-all-done.3 = bf16[8,1,96,1024]{3,2,1,0:T(8,128)(2,1)S(1)} async-done(((bf16[8,1,96,1024]{3,2,1,0:T(8,128)(2,1)}), bf16[8,1,96,1024]{3,2,1,0:T(8,128)(2,1)S(1)}, u32[]{:S(2)}, u32[]{:S(2)}) %all-to-all-start.3) | async-done | bytes 1572896 | tf_op jit(solution)/shard_map/all_to_all | solution.py:87
  180.0 5.4 %all-to-all-start.1 = ((bf16[8,1,96,1024]{3,2,1,0:T(8,128)(2,1)}), bf16[8,1,96,1024]{3,2,1,0:T(8,128)(2,1)}, u32[]{:S(2)}, u32[]{:S(2)}) async-start(bf16[8,1,96,1024]{3,2,1,0:T(8,128)(2,1)} %fusion.47), calls=%async_computation.1 | async-start | bytes 3145728 | tf_op jit(solution)/shard_map/all_to_all | solution.py:68
  185.4 0.3 collective-permute-start.2
  185.7 0.6 fusion.58
  187.6 2.1 gather_fusion.4
  189.7 1.2 gather.32
  190.9 41.2 %all-to-all-done.1 = bf16[8,1,96,1024]{3,2,1,0:T(8,128)(2,1)} async-done(((bf16[8,1,96,1024]{3,2,1,0:T(8,128)(2,1)}), bf16[8,1,96,1024]{3,2,1,0:T(8,128)(2,1)}, u32[]{:S(2)}, u32[]{:S(2)}) %all-to-all-start.1) | async-done | bytes 1572896 | tf_op jit(solution)/shard_map/all_to_all | solution.py:68
  232.2 5.1 %gather_fusion.1 = bf16[512,1024]{1,0:T(8,128)(2,1)} fusion(bf16[768,1024]{1,0:T(8,128)(2,1)} %bitcast.26, s32[1024]{0:T(1024)S(1)} %pad_clamp_fusion.1), kind=kCustom, calls=%fused_computation.1 | custom fusion | bytes 2099200 | tf_op jit(solution)/shard_map/gather | solution.py:71
  237.2 2.4 reshape.244
  239.6 4.6 %reduce_sum.32 = bf16[256,1024]{1,0:T(8,128)(2,1)} reduce(bf16[256,2,1024]{2,1,0:T(2,128)(2,1)} %gather.32, bf16[]{:T(256)} %constant.96.clone.1), dimensions={1}, to_apply=%region_5.6 | reduce | flops 262144 | bytes 1572866 | tf_op jit(solution)/shard_map/reduce_sum | solution.py:90
  244.2 3.5 %multiply_reduce_fusion = bf16[256,1024]{1,0:T(8,128)(2,1)} fusion(f32[256,2,1024]{2,1,0:T(2,128)S(1)} %reshape.244, f32[256,2]{1,0:T(8,128)S(1)} %copy.24), kind=kLoop, calls=%fused_computation.40 | loop fusion | flops 786432 | bytes 2623488 | tf_op jit(solution)/shard_map/reduce_sum | solution.py:72
  247.7 2.4 collective-permute-start
  250.0 2.2 convert_select_fusion
  252.2 28.3 %collective-permute-done.1 = bf16[1,256,1024]{2,1,0:T(8,128)(2,1)} collective-permute-done((bf16[1,256,1024]{2,1,0:T(8,128)(2,1)}, bf16[1,256,1024]{2,1,0:T(8,128)(2,1)}, u32[]{:S(2)}, u32[]{:S(2)}) %collective-permute-start.1) | collective-permute-done | bytes 524320 | tf_op jit(solution)/shard_map/ppermute | solution.py:8
  280.5 2.2 convert_select_fusion.1
  282.7 8.9 %collective-permute-done = bf16[1,256,1024]{2,1,0:T(8,128)(2,1)S(1)} collective-permute-done((bf16[1,256,1024]{2,1,0:T(8,128)(2,1)}, bf16[1,256,1024]{2,1,0:T(8,128)(2,1)S(1)}, u32[]{:S(2)}, u32[]{:S(2)}) %collective-permute-start) | collective-permute-done | bytes 524320 | tf_op jit(solution)/shard_map/ppermute | solution.py:8
  291.6 1.2 convert_select_fusion.2
  (39 shorter events, 0.1 us)
Async XLA Ops:
  7.2 7.6 %copy-start = (bf16[256,1024]{1,0:T(8,128)(2,1)S(1)}, bf16[256,1024]{1,0:T(8,128)(2,1)}, u32[]{:S(2)}) copy-start(bf16[256,1024]{1,0:T(8,128)(2,1)} %param.8) | copy-start | bytes 1572868
  7.2 69.6 %all-gather.4.cloned.1.call-start = ((), (), s32[]{:S(2)}) async-start(), calls=%async_computation.7 | async-start | bytes 2621440 | tf_op jit(solution)/shard_map/all_gather | solution.py:58
  7.9 73.9 %all-gather.6.cloned.1.call-start = ((), (), s32[]{:S(2)}) async-start(), calls=%async_computation.8 | async-start | bytes 2621440 | tf_op jit(solution)/shard_map/all_gather | solution.py:59
  14.8 2.8 copy-start.1
  17.6 3.6 %copy-start.6 = (f32[256,2]{0,1:T(2,128)S(1)}, f32[256,2]{0,1:T(2,128)}, u32[]{:S(2)}) copy-start(f32[256,2]{0,1:T(2,128)} %param.10) | copy-start | bytes 6148
  30.5 40.8 %all-to-all-start = ((bf16[8,1,96,1024]{3,2,1,0:T(8,128)(2,1)}), bf16[8,1,96,1024]{3,2,1,0:T(8,128)(2,1)S(1)}, u32[]{:S(2)}, u32[]{:S(2)}) async-start(bf16[8,1,96,1024]{3,2,1,0:T(8,128)(2,1)} %get-tuple-element.33), calls=%async_computation | async-start | bytes 3145728 | tf_op jit(solution)/shard_map/all_to_all | solution.py:56
  35.9 76.3 %all-gather.8.cloned.1.call-start = ((), (), s32[]{:S(2)}) async-start(), calls=%async_computation.9 | async-start | bytes 2621440 | tf_op jit(solution)/shard_map/all_gather | solution.py:60
  71.3 55.2 %copy-start.2 = (bf16[8,1,96,1024]{3,2,1,0:T(8,128)(2,1)}, bf16[8,1,96,1024]{3,2,1,0:T(8,128)(2,1)S(1)}, u32[]{:S(2)}) copy-start(bf16[8,1,96,1024]{3,2,1,0:T(8,128)(2,1)S(1)} %all-to-all-done) | copy-start | bytes 4718596
  71.3 40.9 %all-to-all-start.2 = ((bf16[8,1,96,1024]{3,2,1,0:T(8,128)(2,1)}), bf16[8,1,96,1024]{3,2,1,0:T(8,128)(2,1)}, u32[]{:S(2)}, u32[]{:S(2)}) async-start(bf16[8,1,96,1024]{3,2,1,0:T(8,128)(2,1)} %get-tuple-element.32), calls=%async_computation.2 | async-start | bytes 3145728 | tf_op jit(solution)/shard_map/all_to_all | solution.py:75
  76.7 108.7 %reduce-scatter.8.cloned.1.call-start = ((), (), s32[]{:S(2)}) async-start(), calls=%async_computation.12 | async-start | bytes 2621440 | tf_op jit(solution)/shard_map/reduce_scatter | solution.py:104
  120.7 1.2 copy-start.11
  126.4 117.7 %reduce-scatter.6.cloned.1.call-start = ((), (), s32[]{:S(2)}) async-start(), calls=%async_computation.11 | async-start | bytes 2621440 | tf_op jit(solution)/shard_map/reduce_scatter | solution.py:101
  131.1 1.6 copy-start.9
  132.7 3.5 %copy-start.8 = (bf16[1,1024,1024]{2,1,0:T(8,128)(2,1)S(1)}, bf16[1,1024,1024]{2,1,0:T(8,128)(2,1)}, u32[]{:S(2)}) copy-start(bf16[1,1024,1024]{2,1,0:T(8,128)(2,1)} %all-gather.4.cloned.1.call-done) | copy-start | bytes 6291460
  132.7 3.5 %copy-start.10 = (bf16[8,1,96,1024]{3,2,0,1:T(8,128)(2,1)S(1)}, bf16[8,1,96,1024]{3,2,0,1:T(8,128)(2,1)}, u32[]{:S(2)}) copy-start(bf16[8,1,96,1024]{3,2,0,1:T(8,128)(2,1)} %get-tuple-element.27) | copy-start | bytes 4718596
  139.2 40.8 %all-to-all-start.3 = ((bf16[8,1,96,1024]{3,2,1,0:T(8,128)(2,1)}), bf16[8,1,96,1024]{3,2,1,0:T(8,128)(2,1)S(1)}, u32[]{:S(2)}, u32[]{:S(2)}) async-start(bf16[8,1,96,1024]{3,2,1,0:T(8,128)(2,1)} %fusion.29), calls=%async_computation.3 | async-start | bytes 3145728 | tf_op jit(solution)/shard_map/all_to_all | solution.py:87
  144.6 103.1 %reduce-scatter.4.cloned.1.call-start = ((), (), s32[]{:S(2)}) async-start(), calls=%async_computation.10 | async-start | bytes 2621440 | tf_op jit(solution)/shard_map/reduce_scatter | solution.py:98
  154.8 30.9 %copy-start.7 = (s32[8]{0:T(128)S(1)}, s32[8]{0:T(128)}, u32[]{:S(2)}) copy-start(s32[8]{0:T(128)} %param.14) | copy-start | bytes 100
  180.0 52.2 %all-to-all-start.1 = ((bf16[8,1,96,1024]{3,2,1,0:T(8,128)(2,1)}), bf16[8,1,96,1024]{3,2,1,0:T(8,128)(2,1)}, u32[]{:S(2)}, u32[]{:S(2)}) async-start(bf16[8,1,96,1024]{3,2,1,0:T(8,128)(2,1)} %fusion.47), calls=%async_computation.1 | async-start | bytes 3145728 | tf_op jit(solution)/shard_map/all_to_all | solution.py:68
  185.4 64.6 %collective-permute-start.2 = (bf16[1,256,1024]{2,1,0:T(8,128)(2,1)}, bf16[1,256,1024]{2,1,0:T(8,128)(2,1)}, u32[]{:S(2)}, u32[]{:S(2)}) collective-permute-start(bf16[1,256,1024]{2,1,0:T(8,128)(2,1)} %reduce-scatter.8.cloned.1.call-done), channel_id=1, source_target_pairs={{0,16},{4,20},{8,24},{12,28},{16,0},{20,4},{24,8},{28,12},{1,17},{... | collective-permute-start | bytes 1572872 | tf_op jit(solution)/shard_map/ppermute | solution.py:8
  244.2 5.8 %copy-start.3 = (bf16[1,256,1024]{2,1,0:T(8,128)(2,1)S(1)}, bf16[1,256,1024]{2,1,0:T(8,128)(2,1)}, u32[]{:S(2)}) copy-start(bf16[1,256,1024]{2,1,0:T(8,128)(2,1)} %reduce-scatter.8.cloned.1.call-done) | copy-start | bytes 1572868
  244.2 36.3 %collective-permute-start.1 = (bf16[1,256,1024]{2,1,0:T(8,128)(2,1)}, bf16[1,256,1024]{2,1,0:T(8,128)(2,1)}, u32[]{:S(2)}, u32[]{:S(2)}) collective-permute-start(bf16[1,256,1024]{2,1,0:T(8,128)(2,1)} %reduce-scatter.6.cloned.1.call-done), channel_id=1, source_target_pairs={{0,16},{4,20},{8,24},{12,28},{16,0},{20,4},{24,8},{28,12},{1,17},{... | collective-permute-start | bytes 1572872 | tf_op jit(solution)/shard_map/ppermute | solution.py:8
  247.7 32.8 %copy-start.4 = (bf16[1,256,1024]{2,1,0:T(8,128)(2,1)S(1)}, bf16[1,256,1024]{2,1,0:T(8,128)(2,1)}, u32[]{:S(2)}) copy-start(bf16[1,256,1024]{2,1,0:T(8,128)(2,1)} %reduce-scatter.6.cloned.1.call-done) | copy-start | bytes 1572868
  247.7 44.0 %collective-permute-start = (bf16[1,256,1024]{2,1,0:T(8,128)(2,1)}, bf16[1,256,1024]{2,1,0:T(8,128)(2,1)S(1)}, u32[]{:S(2)}, u32[]{:S(2)}) collective-permute-start(bf16[1,256,1024]{2,1,0:T(8,128)(2,1)} %reduce-scatter.4.cloned.1.call-done), channel_id=1, source_target_pairs={{0,16},{4,20},{8,24},{12,28},{16,0},{20,4},{24,8},{28,12},{1,17},{... | collective-permute-start | bytes 1572872 | tf_op jit(solution)/shard_map/ppermute | solution.py:8
  252.2 39.4 %copy-start.5 = (bf16[1,256,1024]{2,1,0:T(8,128)(2,1)S(1)}, bf16[1,256,1024]{2,1,0:T(8,128)(2,1)}, u32[]{:S(2)}) copy-start(bf16[1,256,1024]{2,1,0:T(8,128)(2,1)} %reduce-scatter.4.cloned.1.call-done) | copy-start | bytes 1572868
Sparse Core Ops, SparseCore 0:
  9.5 22.9 all-gather.3
  34.1 22.5 all-gather.5
  58.2 22.5 all-gather.7
  126.6 30.7 reduce-scatter.7
  159.8 31.1 reduce-scatter.5
  193.3 31.1 reduce-scatter.3
where the time goes:
time: 304 us; the launch traced here: 300 us
  waiting for transfers between devices  166 us (55%)
  matrix products  44.3 us (15%)
  local copies, waits for them, and re-layouts  30 us (10%)
  starting transfers between devices  24.5 us (8%)
  other arithmetic  19.4 us (6%)
  between operations  15.6 us (5%)
    all_to_all x1, waiting for transfers between devices, shards(): lax.all_to_all(expert_out, 'expert', split_axis=0, concat_axis=0, tiled=T...  41.2 us
    ppermute x3, waiting for transfers between devices, swapped(): lax.ppermute(shard, axis, [(i, i ^ 1 << stride) for i in range(lax.axis_s...  37.2 us
    all_to_all x1, waiting for transfers between devices, shards(): lax.all_to_all(send_x, 'expert', split_axis=0, concat_axis=0, tiled=True)  34.7 us
    all_to_all x1, waiting for transfers between devices, shards(): lax.all_to_all(send_c, 'expert', split_axis=0, concat_axis=0, tiled=True)  25.4 us
    all_to_all x1, waiting for transfers between devices, shards(): lax.all_to_all(copy_grad, 'expert', split_axis=0, concat_axis=0, tiled=True)  25.2 us
    dot_general x1, matrix products, shards(): jnp.einsum('secd,efd->secf', recv_c, full_down, preferred_element_type=jn...  8.45 us
  transfers between devices with their start and end apart: 13, of which 6 were waited for; matrix products, arithmetic and copies ran while one was open for 26% of the time, Pallas kernels for 0%

commit v1 on v0

v1 whole, which is shorter than its diff:
```python
import jax
import jax.numpy as jnp
from jax import lax
from jax.sharding import Mesh, PartitionSpec as P

BF = jnp.bfloat16
F32 = jnp.float32


def flip(value, axis):
    return lax.ppermute(value, axis, [(0, 1), (1, 0)])


def flip_bit(value, axis, bit):
    size = lax.axis_size(axis)
    return lax.ppermute(value, axis, [(i, i ^ (1 << bit)) for i in range(size)])


def pick_two(first, low, high):
    return jnp.where(first, low, high), jnp.where(first, high, low)


def gather_weight(shard, half, side, rest):
    other = flip(shard, "h")
    same = half == side
    keep, send = pick_two(same, shard, other)
    got = flip(send, "b")
    low, high = pick_two(side == 0, keep, got)
    rows, cols = shard.shape
    block = jnp.stack([low, high])[:, None]
    size = lax.axis_size("r")
    for bit in range(size.bit_length() - 1):
        came = flip_bit(block, "r", bit)
        upper = (rest >> bit) & 1
        first, second = pick_two(upper == 0, block, came)
        block = jnp.concatenate([first, second], axis=1)
    return block.reshape(2 * size * rows, cols)


def reduce_grad(partial, half, side, rest, paired):
    size = lax.axis_size("r")
    rows = partial.shape[0] // (2 * size)
    block = partial.reshape(2, size, rows, partial.shape[1])
    for bit in reversed(range(size.bit_length() - 1)):
        upper = (rest >> bit) & 1
        low, high = jnp.split(block, 2, axis=1)
        mine, send = pick_two(upper == 0, low, high)
        came = flip_bit(send, "r", bit)
        block = (mine.astype(F32) + came.astype(F32)).astype(BF)
    block = block[:, 0]
    mine, send = pick_two(side == 0, block[0], block[1])
    came = flip(send, "b")
    final_side = jnp.where(paired, 1 - half, half)
    keep, send = pick_two(side == final_side, mine, came)
    return keep.astype(F32) + flip(send, "h").astype(F32)


def dot(a, b, a_dim, b_dim, kind=F32):
    return lax.dot_general(a, b, (((a_dim,), (b_dim,)), ((), ())), preferred_element_type=kind)


def shards(tokens, route_ids, gate_values, w_gate, w_up, w_down, swap_flags, out_grad):
    half, l_index = lax.axis_index("h"), lax.axis_index("l")
    side, rest = lax.axis_index("b"), lax.axis_index("r")
    half_axis = lax.axis_size("l")
    experts = 2 * half_axis
    tok_rows, width = tokens.shape
    top_k = route_ids.shape[1]
    slot_cap = 3 * tok_rows * top_k // (2 * experts)
    total_slots = experts * slot_cap
    paired = jnp.take(swap_flags, l_index) != jnp.take(swap_flags, l_index + half_axis)

    full_gate = gather_weight(w_gate[0], half, side, rest)
    full_up = gather_weight(w_up[0], half, side, rest)
    full_down = gather_weight(w_down[0], half, side, rest)

    matches = [
        route_ids[:, k, None] == jnp.arange(experts, dtype=jnp.int32)[None] for k in range(top_k)
    ]
    named = sum(match.astype(BF) for match in matches)
    earlier = jnp.tril(jnp.ones((tok_rows, tok_rows), BF), -1)
    before = dot(earlier, named, 1, 0)
    slot_ids = jnp.arange(total_slots, dtype=jnp.int32)[None]
    selected = []
    for k in range(top_k):
        rank = jnp.sum(jnp.where(matches[k], before, 0.0), axis=1).astype(jnp.int32)
        selected.append((route_ids[:, k] * slot_cap + rank)[:, None] == slot_ids)
    chosen = [one.astype(BF) for one in selected]
    picks = sum(chosen)
    slot_gate = sum(
        jnp.sum(jnp.where(selected[k], gate_values[:, k, None], 0.0), axis=0) for k in range(top_k)
    )

    def exchange(rows):
        return lax.all_to_all(
            rows.reshape(experts, slot_cap, width),
            ("b", "l"),
            split_axis=0,
            concat_axis=0,
            tiled=True,
        ).reshape(total_slots, width)

    send_x = dot(picks, tokens, 0, 0, BF)
    send_c = (slot_gate[:, None] * dot(picks, out_grad, 0, 0)).astype(BF)
    recv_x = exchange(send_x)
    recv_c = exchange(send_c)

    pre_gate = dot(recv_x, full_gate, 1, 0)
    pre_up = dot(recv_x, full_up, 1, 0)
    hidden = (jax.nn.silu(pre_gate) * pre_up).astype(BF)
    dw_down = dot(hidden, recv_c, 0, 0).astype(BF)
    grad_down = reduce_grad(dw_down, half, side, rest, paired)
    grad_h = dot(recv_c, full_down, 1, 1)
    sigmoid_a = jax.nn.sigmoid(pre_gate)
    grad_a = (grad_h * pre_up * sigmoid_a * (1.0 + pre_gate * (1.0 - sigmoid_a))).astype(BF)
    grad_b = (grad_h * pre_gate * sigmoid_a).astype(BF)
    grad_gate = reduce_grad(dot(recv_x, grad_a, 0, 0).astype(BF), half, side, rest, paired)
    grad_up = reduce_grad(dot(recv_x, grad_b, 0, 0).astype(BF), half, side, rest, paired)

    expert_out = dot(hidden, full_down, 1, 0).astype(BF)
    returned_out = exchange(expert_out)
    layer_out = sum(
        gate_values[:, k, None] * dot(chosen[k], returned_out, 1, 0) for k in range(top_k)
    ).astype(BF)
    copy_grad = (dot(grad_a, full_gate, 1, 1) + dot(grad_b, full_up, 1, 1)).astype(BF)
    returned_grad = exchange(copy_grad)
    grad_tokens = dot(picks, returned_grad, 1, 0).astype(BF)
    return layer_out, grad_tokens, grad_gate[None], grad_up[None], grad_down[None]


def solution(mesh):
    n_expert, n_dp = mesh.shape["expert"], mesh.shape["dp"]
    split = Mesh(mesh.devices.reshape(2, n_expert // 2, 2, n_dp // 2), ("h", "l", "b", "r"))
    rows = P(("h", "l", "b", "r"), None)
    weight = P(("h", "l"), ("b", "r"), None)
    return jax.shard_map(
        shards,
        mesh=split,
        in_specs=(rows, rows, rows, weight, weight, weight, P(), rows),
        out_specs=(rows, rows, weight, weight, weight),
        check_vma=False,
    )
```

time: 304 us -> 282 us (0.928); the launches traced: 300 us -> 281 us
  starting transfers between devices: 24.5 us -> 57.4 us
  local copies, waits for them, and re-layouts: 30 us -> 3.53 us
  waiting for transfers between devices: 166 us -> 147 us
  between operations: 15.6 us -> 2.28 us
  other arithmetic: 19.4 us -> 24.7 us
    all_to_all x4, waiting for transfers between devices: 126 us -> 0.01 us  [exchange(): lax.all_to_all(rows.reshape(experts, slot_cap, width), ('b', 'l'), split_...]
    ppermute x3 -> x18, waiting for transfers between devices: 37.2 us -> 147 us  [the longest x12 147 us: flip(): return lax.ppermute(value, axis, [(0, 1), (1, 0)])]
    ppermute x3 -> x18, starting transfers between devices: 2.64 us -> 38.7 us  [the longest x6 32.3 us: flip_bit(): return lax.ppermute(value, axis, [(i, i ^ 1 << bit) for i in range(size)])]
    gather x6 -> x0, local copies, waits for them, and re-layouts: 19.8 us -> none  [the longest x1 5.08 us: shards(): returned_out[slot_index].astype(jnp.float32) * weights_flat[:, None]]
    reduce_sum x3 -> x1, other arithmetic: 8.13 us -> 0.24 us  [shards(): jnp.sum(jnp.where(selected[k], gate_values[:, k, None], 0.0), axis=0)]
    broadcast_in_dim x0 -> x6, other arithmetic: none -> 7.1 us  [the longest x3 3.19 us: gather_weight(): block = jnp.stack([low, high])[:, None]]
    convert_element_type x1 -> x5, other arithmetic: 0.01 us -> 3.75 us  [the longest x3 3.74 us: reduce_grad(): block = (mine.astype(F32) + came.astype(F32)).astype(BF)]
    concatenate x0 -> x3, other arithmetic: none -> 3.26 us  [gather_weight(): block = jnp.concatenate([first, second], axis=1)]
  transfers between devices with their start and end apart: 13 -> 22, of which waited for: 6 -> 9; matrix products, arithmetic and copies ran while one was open for 26% -> 19% of each run, Pallas kernels for 0% -> 0%
where the time goes in v1:
time: 282 us; the launch traced here: 281 us
  waiting for transfers between devices  147 us (52%)
  starting transfers between devices  57.4 us (20%)
  matrix products  46.2 us (16%)
  other arithmetic  24.7 us (9%)
  local copies, waits for them, and re-layouts  3.53 us (1%)
    ppermute x12, waiting for transfers between devices, flip(): return lax.ppermute(value, axis, [(0, 1), (1, 0)])  147 us
    dot_general x15, matrix products, dot(): lax.dot_general(a, b, (((a_dim,), (b_dim,)), ((), ())), preferred_element...  46.2 us
    ppermute x6, starting transfers between devices, flip_bit(): return lax.ppermute(value, axis, [(i, i ^ 1 << bit) for i in range(size)])  32.3 us
    all_to_all x4, starting transfers between devices, exchange(): lax.all_to_all(rows.reshape(experts, slot_cap, width), ('b', 'l'), split_...  18.7 us
    select_n x14, other arithmetic, pick_two(): return (jnp.where(first, low, high), jnp.where(first, high, low))  8.31 us
    ppermute x12, starting transfers between devices, flip(): return lax.ppermute(value, axis, [(0, 1), (1, 0)])  6.32 us
  transfers between devices with their start and end apart: 22, of which 9 were waited for; matrix products, arithmetic and copies ran while one was open for 19% of the time, Pallas kernels for 0%

profile of v1, /device:TPU:31, one launch (start us, length us, event | category | flops | bytes accessed | tf_op | source)
XLA Modules:
  0.0 281.1 jit_solution(807388809655666758)
XLA Ops:
  0.7 0.8 fusion.33
  1.4 0.3 select_reduce_fusion.3
  1.7 0.8 multiply_add_fusion.1
  2.5 2.0 fusion.7
  4.5 4.7 %all-to-all-start = ((bf16[8,96,1024]{2,1,0:T(8,128)(2,1)}), bf16[8,96,1024]{2,1,0:T(8,128)(2,1)}, u32[]{:S(2)}, u32[]{:S(2)}) async-start(bf16[8,96,1024]{2,1,0:T(8,128)(2,1)} %bitcast.138), calls=%async_computation | async-start | bytes 3145728 | tf_op jit(solution)/shard_map/all_to_all | solution.py:95
  9.2 2.3 collective-permute-start.3
  11.6 0.2 select_reduce_fusion
  11.9 3.0 %multiply_convert_fusion.2 = bf16[768,1024]{1,0:T(8,128)(2,1)} fusion(bf16[256,1024]{1,0:T(8,128)(2,1)} %param.15, f32[768]{0:T(1024)S(1)} %add.82, s32[256]{0:T(256)S(1)} %bitcast.147, s32[256]{0:T(256)S(1)} %bitcast.142), kind=kOutput, calls=%fused_computation.3 | convolution fusion | flops 405798912 | bytes 2102272 | tf_op jit(solution)/shard_map/dot_general | solution.py:59
  14.8 52.5 %collective-permute-done.3 = bf16[256,1024]{1,0:T(8,128)(2,1)S(1)} collective-permute-done((bf16[256,1024]{1,0:T(8,128)(2,1)S(1)}, bf16[256,1024]{1,0:T(8,128)(2,1)S(1)}, u32[]{:S(2)}, u32[]{:S(2)}) %collective-permute-start.3) | collective-permute-done | bytes 524320 | tf_op jit(solution)/shard_map/ppermute | solution.py:11
  67.4 0.3 collective-permute-start.4
  67.8 1.2 collective-permute-start.7
  69.1 9.5 %collective-permute-done = bf16[256,1024]{1,0:T(8,128)(2,1)S(1)} collective-permute-done((bf16[256,1024]{1,0:T(8,128)(2,1)S(1)}, bf16[256,1024]{1,0:T(8,128)(2,1)S(1)}, u32[]{:S(2)}, u32[]{:S(2)}) %collective-permute-start) | collective-permute-done | bytes 524320 | tf_op jit(solution)/shard_map/ppermute | solution.py:11
  78.6 0.9 broadcast_select_fusion.14
  79.5 0.3 collective-permute-start.1
  79.9 1.1 maximum_bitcast_fusion.1
  81.0 6.2 %collective-permute-start.5 = (bf16[2,1,256,1024]{3,2,0,1:T(8,128)(2,1)}, bf16[2,1,256,1024]{3,2,0,1:T(8,128)(2,1)}, u32[]{:S(2)}, u32[]{:S(2)}) collective-permute-start(bf16[2,1,256,1024]{3,2,0,1:T(8,128)(2,1)} %maximum_bitcast_fusion.1), channel_id=1, source_target_pairs={{0,1},{1,0},{2,3},{3,2},{4,5},{5,4},{6,7},{7,6},{8,9},{9,8},{10,11... | collective-permute-start | bytes 3145736 | tf_op jit(solution)/shard_map/ppermute | solution.py:16
  87.1 1.4 collective-permute-done.7
  88.6 4.6 %all-to-all-start.2 = ((bf16[8,96,1024]{2,1,0:T(8,128)(2,1)}), bf16[8,96,1024]{2,1,0:T(8,128)(2,1)}, u32[]{:S(2)}, u32[]{:S(2)}) async-start(bf16[8,96,1024]{2,1,0:T(8,128)(2,1)} %bitcast.136), calls=%async_computation.2 | async-start | bytes 3145728 | tf_op jit(solution)/shard_map/all_to_all | solution.py:95
  93.2 1.1 maximum_bitcast_fusion.2
  94.2 15.6 %collective-permute-start.8 = (bf16[2,1,256,1024]{3,2,1,0:T(8,128)(2,1)}, bf16[2,1,256,1024]{3,2,1,0:T(8,128)(2,1)}, u32[]{:S(2)}, u32[]{:S(2)}) collective-permute-start(bf16[2,1,256,1024]{3,2,1,0:T(8,128)(2,1)} %maximum_bitcast_fusion.2), channel_id=1, source_target_pairs={{0,1},{1,0},{2,3},{3,2},{4,5},{5,4},{6,7},{7,6},{8,9},{9,8},{10,11... | collective-permute-start | bytes 3145736 | tf_op jit(solution)/shard_map/ppermute | solution.py:16
  109.8 1.1 select_bitcast_fusion.8
  111.0 1.1 maximum_bitcast_fusion
  112.0 9.3 %collective-permute-start.2 = (bf16[2,1,256,1024]{3,2,1,0:T(8,128)(2,1)}, bf16[2,1,256,1024]{3,2,1,0:T(8,128)(2,1)}, u32[]{:S(2)}, u32[]{:S(2)}) collective-permute-start(bf16[2,1,256,1024]{3,2,1,0:T(8,128)(2,1)} %maximum_bitcast_fusion), channel_id=1, source_target_pairs={{0,1},{1,0},{2,3},{3,2},{4,5},{5,4},{6,7},{7,6},{8,9},{9,8},{10,11... | collective-permute-start | bytes 3145736 | tf_op jit(solution)/shard_map/ppermute | solution.py:16
  121.4 0.6 fusion.34
  123.3 1.4 bitcast_select_fusion.1
  125.0 2.6 broadcast_select_fusion.3
  127.6 1.5 pad_maximum_fusion.2
  129.1 1.6 pad_maximum_fusion
  130.7 4.8 %fusion.35 = f32[768,1024]{1,0:T(8,128)} fusion(bf16[768,1024]{1,0:T(8,128)(2,1)} %bitcast.8, bf16[1024,1024]{1,0:T(8,128)(2,1)S(1)} %bitcast.130), kind=kOutput, calls=%fused_computation.99 | convolution fusion | flops 1610612736 | bytes 6815744 | tf_op jit(solution)/shard_map/dot_general | solution.py:59
  135.5 4.0 %fusion.36 = f32[768,1024]{1,0:T(8,128)S(1)} fusion(bf16[768,1024]{1,0:T(8,128)(2,1)} %bitcast.30, bf16[1024,1024]{1,0:T(8,128)(2,1)} %bitcast.134), kind=kOutput, calls=%fused_computation.100 | convolution fusion | flops 1610612736 | bytes 6815744 | tf_op jit(solution)/shard_map/dot_general | solution.py:59
  139.6 6.2 %multiply_convert_fusion.1 = (bf16[768,1024]{1,0:T(8,128)(2,1)}, bf16[768,1024]{1,0:T(8,128)(2,1)S(1)}, bf16[768,1024]{1,0:T(8,128)(2,1)}) fusion(f32[768,1024]{1,0:T(8,128)S(1)} %fusion.36, f32[768,1024]{1,0:T(8,128)S(1)} %copy-done.16, bf16[768,1024]{1,0:T(8,128)(2,1)} %bitcast.8, bf16[1024,1024]{1,0:T(8,128)(2,1)S(1)} %bitcast.132), kind=kOutput, calls=%fused_computation.2 | convolution fusion | flops 1623195648 | bytes 14680064 | tf_op jit(solution)/shard_map/dot_general | solution.py:59
  145.8 2.9 %convolution_convert_fusion.3 = bf16[768,1024]{1,0:T(8,128)(2,1)} fusion(bf16[768,1024]{1,0:T(8,128)(2,1)S(1)} %get-tuple-element.30, bf16[1024,1024]{1,0:T(8,128)(2,1)S(1)} %bitcast.135), kind=kOutput, calls=%fused_computation.17 | convolution fusion | flops 1611399168 | bytes 5242880 | tf_op jit(solution)/shard_map/dot_general | solution.py:59
  148.7 4.5 %all-to-all-start.1 = ((bf16[8,96,1024]{2,1,0:T(8,128)(2,1)}), bf16[8,96,1024]{2,1,0:T(8,128)(2,1)}, u32[]{:S(2)}, u32[]{:S(2)}) async-start(bf16[8,96,1024]{2,1,0:T(8,128)(2,1)} %bitcast.139), calls=%async_computation.1 | async-start | bytes 3145728 | tf_op jit(solution)/shard_map/all_to_all | solution.py:95
  153.3 3.8 %convolution_convert_fusion.2 = bf16[1024,1024]{1,0:T(8,128)(2,1)S(1)} fusion(bf16[768,1024]{1,0:T(8,128)(2,1)} %bitcast.8, bf16[768,1024]{1,0:T(8,128)(2,1)} %get-tuple-element.29), kind=kOutput, calls=%fused_computation.16 | convolution fusion | flops 1611661312 | bytes 5242880 | tf_op jit(solution)/shard_map/dot_general | solution.py:59
  157.1 3.2 %convolution_convert_fusion.1 = bf16[1024,1024]{1,0:T(8,128)(2,1)S(1)} fusion(bf16[768,1024]{1,0:T(8,128)(2,1)} %bitcast.8, bf16[768,1024]{1,0:T(8,128)(2,1)S(1)} %copy-done.18), kind=kOutput, calls=%fused_computation.15 | convolution fusion | flops 1611661312 | bytes 5242880 | tf_op jit(solution)/shard_map/dot_general | solution.py:59
  160.6 0.6 collective-permute-start.12
  161.3 0.6 copy-done.20
  161.9 3.3 %convolution_convert_fusion = bf16[1024,1024]{1,0:T(8,128)(2,1)S(1)} fusion(bf16[768,1024]{1,0:T(8,128)(2,1)S(1)} %copy-done.20, bf16[768,1024]{1,0:T(8,128)(2,1)} %bitcast.30), kind=kOutput, calls=%fused_computation.14 | convolution fusion | flops 1611661312 | bytes 5242880 | tf_op jit(solution)/shard_map/dot_general | solution.py:59
  165.2 1.3 copy-done.2
  166.5 1.1 broadcast_select_fusion.4
  167.6 0.6 collective-permute-start.15
  168.2 1.8 fusion.37
  170.0 3.0 %add_convert_fusion = bf16[768,1024]{1,0:T(8,128)(2,1)} fusion(f32[768,1024]{1,0:T(8,128)S(1)} %fusion.37, bf16[768,1024]{1,0:T(8,128)(2,1)S(1)} %copy-done.17, bf16[1024,1024]{1,0:T(8,128)(2,1)S(1)} %bitcast.133), kind=kOutput, calls=%fused_computation | convolution fusion | flops 1612185600 | bytes 8388608 | tf_op jit(solution)/shard_map/dot_general | solution.py:59
  173.0 0.6 add_convert_fusion.2
  173.7 0.9 select_bitcast_fusion.1
  174.5 0.3 collective-permute-start.13
  174.8 0.6 add_convert_fusion.3
  175.4 0.9 select_bitcast_fusion.2
  176.3 1.2 collective-permute-start.10
  177.5 5.0 %all-to-all-start.3 = ((bf16[8,96,1024]{2,1,0:T(8,128)(2,1)}), bf16[8,96,1024]{2,1,0:T(8,128)(2,1)}, u32[]{:S(2)}, u32[]{:S(2)}) async-start(bf16[8,96,1024]{2,1,0:T(8,128)(2,1)} %bitcast.137), calls=%async_computation.3 | async-start | bytes 3145728 | tf_op jit(solution)/shard_map/all_to_all | solution.py:95
  182.4 2.5 add_convert_fusion.1
  185.0 0.3 collective-permute-start.16
  185.3 15.6 %collective-permute-done.13 = bf16[256,1024]{1,0:T(8,128)(2,1)S(1)} collective-permute-done((bf16[256,1024]{1,0:T(8,128)(2,1)}, bf16[256,1024]{1,0:T(8,128)(2,1)S(1)}, u32[]{:S(2)}, u32[]{:S(2)}) %collective-permute-start.13) | collective-permute-done | bytes 524320 | tf_op jit(solution)/shard_map/ppermute | solution.py:11
  201.1 11.0 %collective-permute-done.10 = bf16[256,1024]{1,0:T(8,128)(2,1)S(1)} collective-permute-done((bf16[256,1024]{1,0:T(8,128)(2,1)}, bf16[256,1024]{1,0:T(8,128)(2,1)S(1)}, u32[]{:S(2)}, u32[]{:S(2)}) %collective-permute-start.10) | collective-permute-done | bytes 524320 | tf_op jit(solution)/shard_map/ppermute | solution.py:11
  212.2 15.3 %collective-permute-done.16 = bf16[256,1024]{1,0:T(8,128)(2,1)S(1)} collective-permute-done((bf16[256,1024]{1,0:T(8,128)(2,1)S(1)}, bf16[256,1024]{1,0:T(8,128)(2,1)S(1)}, u32[]{:S(2)}, u32[]{:S(2)}) %collective-permute-start.16) | collective-permute-done | bytes 524320 | tf_op jit(solution)/shard_map/ppermute | solution.py:11
  227.7 21.8 %collective-permute-done.14 = bf16[256,1024]{1,0:T(8,128)(2,1)S(1)} collective-permute-done((bf16[256,1024]{1,0:T(8,128)(2,1)S(1)}, bf16[256,1024]{1,0:T(8,128)(2,1)S(1)}, u32[]{:S(2)}, u32[]{:S(2)}) %collective-permute-start.14) | collective-permute-done | bytes 524320 | tf_op jit(solution)/shard_map/ppermute | solution.py:11
  249.5 1.3 add_bitcast_fusion.1
  250.8 9.9 %collective-permute-done.11 = bf16[256,1024]{1,0:T(8,128)(2,1)S(1)} collective-permute-done((bf16[256,1024]{1,0:T(8,128)(2,1)S(1)}, bf16[256,1024]{1,0:T(8,128)(2,1)S(1)}, u32[]{:S(2)}, u32[]{:S(2)}) %collective-permute-start.11) | collective-permute-done | bytes 524320 | tf_op jit(solution)/shard_map/ppermute | solution.py:11
  260.7 1.3 add_bitcast_fusion.2
  262.0 9.9 %collective-permute-done.17 = bf16[256,1024]{1,0:T(8,128)(2,1)S(1)} collective-permute-done((bf16[256,1024]{1,0:T(8,128)(2,1)S(1)}, bf16[256,1024]{1,0:T(8,128)(2,1)S(1)}, u32[]{:S(2)}, u32[]{:S(2)}) %collective-permute-start.17) | collective-permute-done | bytes 524320 | tf_op jit(solution)/shard_map/ppermute | solution.py:11
  272.0 1.3 add_bitcast_fusion
  273.3 2.0 convolution_multiply_fusion.1
  275.3 2.9 %fusion.1 = bf16[256,1024]{1,0:T(8,128)(2,1)} fusion(f32[256,1024]{1,0:T(8,128)S(1)} %convolution_multiply_fusion.1, bf16[768,1024]{1,0:T(8,128)(2,1)} %bitcast.27, f32[256]{0:T(256)S(1)} %bitcast.151, s32[256]{0:T(256)S(1)} %bitcast.148), kind=kOutput, calls=%fused_computation.21 | convolution fusion | flops 403636224 | bytes 3147776 | tf_op jit(solution)/shard_map/dot_general | solution.py:59
  278.2 2.9 %convolution_convert_fusion.4 = bf16[256,1024]{1,0:T(8,128)(2,1)} fusion(bf16[768,1024]{1,0:T(8,128)(2,1)} %bitcast.32, s32[256]{0:T(256)S(1)} %bitcast.149, s32[256]{0:T(256)S(1)} %bitcast.144), kind=kOutput, calls=%fused_computation.22 | convolution fusion | flops 404488192 | bytes 2099200 | tf_op jit(solution)/shard_map/dot_general | solution.py:59
  (76 shorter events, 1.8 us)
Async XLA Ops:
  0.6 1.9 copy-start
  4.5 4.7 %copy-start.4 = (bf16[1,256,1024]{2,1,0:T(8,128)(2,1)S(1)}, bf16[1,256,1024]{2,1,0:T(8,128)(2,1)}, u32[]{:S(2)}) copy-start(bf16[1,256,1024]{2,1,0:T(8,128)(2,1)} %param.13) | copy-start | bytes 1572868
  4.5 4.8 %copy-start.3 = (bf16[1,256,1024]{2,1,0:T(8,128)(2,1)S(1)}, bf16[1,256,1024]{2,1,0:T(8,128)(2,1)}, u32[]{:S(2)}) copy-start(bf16[1,256,1024]{2,1,0:T(8,128)(2,1)} %param.12) | copy-start | bytes 1572868
  4.5 7.1 %copy-start.5 = (bf16[1,256,1024]{2,1,0:T(8,128)(2,1)S(1)}, bf16[1,256,1024]{2,1,0:T(8,128)(2,1)}, u32[]{:S(2)}) copy-start(bf16[1,256,1024]{2,1,0:T(8,128)(2,1)} %param.11) | copy-start | bytes 1572868
  4.5 7.1 %copy-start.15 = (f32[256,2]{0,1:T(2,128)S(1)}, f32[256,2]{0,1:T(2,128)}, u32[]{:S(2)}) copy-start(f32[256,2]{0,1:T(2,128)} %param.10) | copy-start | bytes 6148
  4.5 84.1 %all-to-all-start = ((bf16[8,96,1024]{2,1,0:T(8,128)(2,1)}), bf16[8,96,1024]{2,1,0:T(8,128)(2,1)}, u32[]{:S(2)}, u32[]{:S(2)}) async-start(bf16[8,96,1024]{2,1,0:T(8,128)(2,1)} %bitcast.138), calls=%async_computation | async-start | bytes 3145728 | tf_op jit(solution)/shard_map/all_to_all | solution.py:95
  9.2 58.6 %collective-permute-start.6 = (bf16[256,1024]{1,0:T(8,128)(2,1)S(1)}, bf16[256,1024]{1,0:T(8,128)(2,1)S(1)}, u32[]{:S(2)}, u32[]{:S(2)}) collective-permute-start(bf16[256,1024]{1,0:T(8,128)(2,1)S(1)} %bitcast.128), channel_id=1, source_target_pairs={{0,16},{16,0},{1,17},{17,1},{2,18},{18,2},{3,19},{19,3},{4,20},{20... | collective-permute-start | bytes 1572872 | tf_op jit(solution)/shard_map/ppermute | solution.py:11
  9.2 58.1 %collective-permute-start.3 = (bf16[256,1024]{1,0:T(8,128)(2,1)S(1)}, bf16[256,1024]{1,0:T(8,128)(2,1)S(1)}, u32[]{:S(2)}, u32[]{:S(2)}) collective-permute-start(bf16[256,1024]{1,0:T(8,128)(2,1)S(1)} %bitcast.127), channel_id=1, source_target_pairs={{0,16},{16,0},{1,17},{17,1},{2,18},{18,2},{3,19},{19,3},{4,20},{20... | collective-permute-start | bytes 1572872 | tf_op jit(solution)/shard_map/ppermute | solution.py:11
  11.6 67.0 %collective-permute-start = (bf16[256,1024]{1,0:T(8,128)(2,1)S(1)}, bf16[256,1024]{1,0:T(8,128)(2,1)S(1)}, u32[]{:S(2)}, u32[]{:S(2)}) collective-permute-start(bf16[256,1024]{1,0:T(8,128)(2,1)S(1)} %bitcast.129), channel_id=1, source_target_pairs={{0,16},{16,0},{1,17},{17,1},{2,18},{18,2},{3,19},{19,3},{4,20},{20... | collective-permute-start | bytes 1572872 | tf_op jit(solution)/shard_map/ppermute | solution.py:11
  67.4 12.2 %copy-start.9 = (bf16[256,1024]{1,0:T(8,128)(2,1)}, bf16[256,1024]{1,0:T(8,128)(2,1)S(1)}, u32[]{:S(2)}) copy-start(bf16[256,1024]{1,0:T(8,128)(2,1)S(1)} %collective-permute-done.3) | copy-start | bytes 1572868
  67.4 12.4 %collective-permute-start.4 = (bf16[256,1024]{1,0:T(8,128)(2,1)S(1)}, bf16[256,1024]{1,0:T(8,128)(2,1)S(1)}, u32[]{:S(2)}, u32[]{:S(2)}) collective-permute-start(bf16[256,1024]{1,0:T(8,128)(2,1)S(1)} %broadcast_select_fusion.12), channel_id=1, source_target_pairs={{0,2},{2,0},{1,3},{3,1},{4,6},{6,4},{5,7},{7,5},{8,10},{10,8},{9,1... | collective-permute-start | bytes 1572872 | tf_op jit(solution)/shard_map/ppermute | solution.py:11
  67.8 20.7 %collective-permute-start.7 = (bf16[256,1024]{1,0:T(8,128)(2,1)S(1)}, bf16[256,1024]{1,0:T(8,128)(2,1)S(1)}, u32[]{:S(2)}, u32[]{:S(2)}) collective-permute-start(bf16[256,1024]{1,0:T(8,128)(2,1)S(1)} %broadcast_select_fusion.10), channel_id=1, source_target_pairs={{0,2},{2,0},{1,3},{3,1},{4,6},{6,4},{5,7},{7,5},{8,10},{10,8},{9,1... | collective-permute-start | bytes 1572872 | tf_op jit(solution)/shard_map/ppermute | solution.py:11
  78.6 1.2 copy-start.7
  79.5 30.3 %collective-permute-start.1 = (bf16[256,1024]{1,0:T(8,128)(2,1)}, bf16[256,1024]{1,0:T(8,128)(2,1)}, u32[]{:S(2)}, u32[]{:S(2)}) collective-permute-start(bf16[256,1024]{1,0:T(8,128)(2,1)} %broadcast_select_fusion.14), channel_id=1, source_target_pairs={{0,2},{2,0},{1,3},{3,1},{4,6},{6,4},{5,7},{7,5},{8,10},{10,8},{9,1... | collective-permute-start | bytes 1572872 | tf_op jit(solution)/shard_map/ppermute | solution.py:11
  81.0 42.3 %collective-permute-start.5 = (bf16[2,1,256,1024]{3,2,0,1:T(8,128)(2,1)}, bf16[2,1,256,1024]{3,2,0,1:T(8,128)(2,1)}, u32[]{:S(2)}, u32[]{:S(2)}) collective-permute-start(bf16[2,1,256,1024]{3,2,0,1:T(8,128)(2,1)} %maximum_bitcast_fusion.1), channel_id=1, source_target_pairs={{0,1},{1,0},{2,3},{3,2},{4,5},{5,4},{6,7},{7,6},{8,9},{9,8},{10,11... | collective-permute-start | bytes 3145736 | tf_op jit(solution)/shard_map/ppermute | solution.py:16
  88.6 46.9 %all-to-all-start.2 = ((bf16[8,96,1024]{2,1,0:T(8,128)(2,1)}), bf16[8,96,1024]{2,1,0:T(8,128)(2,1)}, u32[]{:S(2)}, u32[]{:S(2)}) async-start(bf16[8,96,1024]{2,1,0:T(8,128)(2,1)} %bitcast.136), calls=%async_computation.2 | async-start | bytes 3145728 | tf_op jit(solution)/shard_map/all_to_all | solution.py:95
  93.2 16.6 %copy-start.6 = (bf16[1,256,1024]{2,1,0:T(8,128)(2,1)S(1)}, bf16[1,256,1024]{2,1,0:T(8,128)(2,1)}, u32[]{:S(2)}) copy-start(bf16[1,256,1024]{2,1,0:T(8,128)(2,1)} %param.11) | copy-start | bytes 1572868
  93.2 16.6 %copy-start.8 = (bf16[256,1024]{1,0:T(8,128)(2,1)S(1)}, bf16[256,1024]{1,0:T(8,128)(2,1)}, u32[]{:S(2)}) copy-start(bf16[256,1024]{1,0:T(8,128)(2,1)} %copy-done.7) | copy-start | bytes 1572868
  94.2 27.1 %copy-start.14 = (s32[8]{0:T(128)S(1)}, s32[8]{0:T(128)}, u32[]{:S(2)}) copy-start(s32[8]{0:T(128)} %param.14) | copy-start | bytes 100
  94.2 30.8 %collective-permute-start.8 = (bf16[2,1,256,1024]{3,2,1,0:T(8,128)(2,1)}, bf16[2,1,256,1024]{3,2,1,0:T(8,128)(2,1)}, u32[]{:S(2)}, u32[]{:S(2)}) collective-permute-start(bf16[2,1,256,1024]{3,2,1,0:T(8,128)(2,1)} %maximum_bitcast_fusion.2), channel_id=1, source_target_pairs={{0,1},{1,0},{2,3},{3,2},{4,5},{5,4},{6,7},{7,6},{8,9},{9,8},{10,11... | collective-permute-start | bytes 3145736 | tf_op jit(solution)/shard_map/ppermute | solution.py:16
  112.0 13.0 %collective-permute-start.2 = (bf16[2,1,256,1024]{3,2,1,0:T(8,128)(2,1)}, bf16[2,1,256,1024]{3,2,1,0:T(8,128)(2,1)}, u32[]{:S(2)}, u32[]{:S(2)}) collective-permute-start(bf16[2,1,256,1024]{3,2,1,0:T(8,128)(2,1)} %maximum_bitcast_fusion), channel_id=1, source_target_pairs={{0,1},{1,0},{2,3},{3,2},{4,5},{5,4},{6,7},{7,6},{8,9},{9,8},{10,11... | collective-permute-start | bytes 3145736 | tf_op jit(solution)/shard_map/ppermute | solution.py:16
  125.0 5.7 %copy-start.10 = (bf16[2,2,256,1024]{3,2,1,0:T(8,128)(2,1)}, bf16[2,2,256,1024]{3,2,1,0:T(8,128)(2,1)S(1)}, u32[]{:S(2)}) copy-start(bf16[2,2,256,1024]{3,2,1,0:T(8,128)(2,1)S(1)} %copy.22) | copy-start | bytes 6291460
  135.5 4.0 %copy-start.12 = (bf16[2,2,256,1024]{3,2,1,0:T(8,128)(2,1)S(1)}, bf16[2,2,256,1024]{3,2,1,0:T(8,128)(2,1)}, u32[]{:S(2)}) copy-start(bf16[2,2,256,1024]{3,2,1,0:T(8,128)(2,1)} %pad_maximum_fusion) | copy-start | bytes 6291460
  135.5 4.1 %copy-start.16 = (f32[768,1024]{1,0:T(8,128)S(1)}, f32[768,1024]{1,0:T(8,128)}, u32[]{:S(2)}) copy-start(f32[768,1024]{1,0:T(8,128)} %fusion.35) | copy-start | bytes 9437188
  139.6 6.2 %copy-start.13 = (bf16[2,2,256,1024]{3,2,1,0:T(8,128)(2,1)S(1)}, bf16[2,2,256,1024]{3,2,1,0:T(8,128)(2,1)}, u32[]{:S(2)}) copy-start(bf16[2,2,256,1024]{3,2,1,0:T(8,128)(2,1)} %pad_maximum_fusion.2) | copy-start | bytes 6291460
  145.8 3.0 %copy-start.19 = (bf16[768,1024]{1,0:T(8,128)(2,1)}, bf16[768,1024]{1,0:T(8,128)(2,1)S(1)}, u32[]{:S(2)}) copy-start(bf16[768,1024]{1,0:T(8,128)(2,1)S(1)} %get-tuple-element.30) | copy-start | bytes 4718596
  148.7 28.7 %all-to-all-start.1 = ((bf16[8,96,1024]{2,1,0:T(8,128)(2,1)}), bf16[8,96,1024]{2,1,0:T(8,128)(2,1)}, u32[]{:S(2)}, u32[]{:S(2)}) async-start(bf16[8,96,1024]{2,1,0:T(8,128)(2,1)} %bitcast.139), calls=%async_computation.1 | async-start | bytes 3145728 | tf_op jit(solution)/shard_map/all_to_all | solution.py:95
  153.3 3.8 %copy-start.18 = (bf16[768,1024]{1,0:T(8,128)(2,1)S(1)}, bf16[768,1024]{1,0:T(8,128)(2,1)}, u32[]{:S(2)}) copy-start(bf16[768,1024]{1,0:T(8,128)(2,1)} %get-tuple-element.31) | copy-start | bytes 4718596
  160.5 1.4 copy-start.20
  160.6 12.4 %collective-permute-start.12 = (bf16[2,1,256,1024]{3,2,1,0:T(8,128)(2,1)S(1)}, bf16[2,1,256,1024]{3,2,1,0:T(8,128)(2,1)S(1)}, u32[]{:S(2)}, u32[]{:S(2)}) collective-permute-start(bf16[2,1,256,1024]{3,2,1,0:T(8,128)(2,1)S(1)} %broadcast_select_fusion), channel_id=1, source_target_pairs={{0,1},{1,0},{2,3},{3,2},{4,5},{5,4},{6,7},{7,6},{8,9},{9,8},{10,11... | collective-permute-start | bytes 3145736 | tf_op jit(solution)/shard_map/ppermute | solution.py:16
  161.3 13.5 %collective-permute-start.9 = (bf16[2,1,256,1024]{3,2,1,0:T(8,128)(2,1)S(1)}, bf16[2,1,256,1024]{3,2,1,0:T(8,128)(2,1)S(1)}, u32[]{:S(2)}, u32[]{:S(2)}) collective-permute-start(bf16[2,1,256,1024]{3,2,1,0:T(8,128)(2,1)S(1)} %broadcast_select_fusion.1), channel_id=1, source_target_pairs={{0,1},{1,0},{2,3},{3,2},{4,5},{5,4},{6,7},{7,6},{8,9},{9,8},{10,11... | collective-permute-start | bytes 3145736 | tf_op jit(solution)/shard_map/ppermute | solution.py:16
  165.2 1.3 copy-start.2
  165.2 3.0 %copy-start.11 = (bf16[2,2,256,1024]{3,2,1,0:T(8,128)(2,1)S(1)}, bf16[2,2,256,1024]{3,2,1,0:T(8,128)(2,1)}, u32[]{:S(2)}) copy-start(bf16[2,2,256,1024]{3,2,1,0:T(8,128)(2,1)} %copy-done.10) | copy-start | bytes 6291460
  167.6 2.4 copy-start.17
  167.6 14.8 %collective-permute-start.15 = (bf16[2,1,256,1024]{3,2,1,0:T(8,128)(2,1)}, bf16[2,1,256,1024]{3,2,1,0:T(8,128)(2,1)}, u32[]{:S(2)}, u32[]{:S(2)}) collective-permute-start(bf16[2,1,256,1024]{3,2,1,0:T(8,128)(2,1)} %broadcast_select_fusion.4), channel_id=1, source_target_pairs={{0,1},{1,0},{2,3},{3,2},{4,5},{5,4},{6,7},{7,6},{8,9},{9,8},{10,11... | collective-permute-start | bytes 3145736 | tf_op jit(solution)/shard_map/ppermute | solution.py:16
  174.5 26.4 %collective-permute-start.13 = (bf16[256,1024]{1,0:T(8,128)(2,1)}, bf16[256,1024]{1,0:T(8,128)(2,1)S(1)}, u32[]{:S(2)}, u32[]{:S(2)}) collective-permute-start(bf16[256,1024]{1,0:T(8,128)(2,1)} %select_bitcast_fusion.1), channel_id=1, source_target_pairs={{0,2},{2,0},{1,3},{3,1},{4,6},{6,4},{5,7},{7,5},{8,10},{10,8},{9,1... | collective-permute-start | bytes 1572872 | tf_op jit(solution)/shard_map/ppermute | solution.py:11
  176.3 35.8 %collective-permute-start.10 = (bf16[256,1024]{1,0:T(8,128)(2,1)}, bf16[256,1024]{1,0:T(8,128)(2,1)S(1)}, u32[]{:S(2)}, u32[]{:S(2)}) collective-permute-start(bf16[256,1024]{1,0:T(8,128)(2,1)} %select_bitcast_fusion.2), channel_id=1, source_target_pairs={{0,2},{2,0},{1,3},{3,1},{4,6},{6,4},{5,7},{7,5},{8,10},{10,8},{9,1... | collective-permute-start | bytes 1572872 | tf_op jit(solution)/shard_map/ppermute | solution.py:11
  177.5 100.7 %all-to-all-start.3 = ((bf16[8,96,1024]{2,1,0:T(8,128)(2,1)}), bf16[8,96,1024]{2,1,0:T(8,128)(2,1)}, u32[]{:S(2)}, u32[]{:S(2)}) async-start(bf16[8,96,1024]{2,1,0:T(8,128)(2,1)} %bitcast.137), calls=%async_computation.3 | async-start | bytes 3145728 | tf_op jit(solution)/shard_map/all_to_all | solution.py:95
  185.0 42.5 %collective-permute-start.16 = (bf16[256,1024]{1,0:T(8,128)(2,1)S(1)}, bf16[256,1024]{1,0:T(8,128)(2,1)S(1)}, u32[]{:S(2)}, u32[]{:S(2)}) collective-permute-start(bf16[256,1024]{1,0:T(8,128)(2,1)S(1)} %select_bitcast_fusion), channel_id=1, source_target_pairs={{0,2},{2,0},{1,3},{3,1},{4,6},{6,4},{5,7},{7,5},{8,10},{10,8},{9,1... | collective-permute-start | bytes 1572872 | tf_op jit(solution)/shard_map/ppermute | solution.py:11
  201.0 48.5 %collective-permute-start.14 = (bf16[256,1024]{1,0:T(8,128)(2,1)S(1)}, bf16[256,1024]{1,0:T(8,128)(2,1)S(1)}, u32[]{:S(2)}, u32[]{:S(2)}) collective-permute-start(bf16[256,1024]{1,0:T(8,128)(2,1)S(1)} %bitcast_select_fusion.4), channel_id=1, source_target_pairs={{0,16},{16,0},{1,17},{17,1},{2,18},{18,2},{3,19},{19,3},{4,20},{20... | collective-permute-start | bytes 1572872 | tf_op jit(solution)/shard_map/ppermute | solution.py:11
  212.1 48.6 %collective-permute-start.11 = (bf16[256,1024]{1,0:T(8,128)(2,1)S(1)}, bf16[256,1024]{1,0:T(8,128)(2,1)S(1)}, u32[]{:S(2)}, u32[]{:S(2)}) collective-permute-start(bf16[256,1024]{1,0:T(8,128)(2,1)S(1)} %bitcast_select_fusion.6), channel_id=1, source_target_pairs={{0,16},{16,0},{1,17},{17,1},{2,18},{18,2},{3,19},{19,3},{4,20},{20... | collective-permute-start | bytes 1572872 | tf_op jit(solution)/shard_map/ppermute | solution.py:11
  227.6 44.3 %collective-permute-start.17 = (bf16[256,1024]{1,0:T(8,128)(2,1)S(1)}, bf16[256,1024]{1,0:T(8,128)(2,1)S(1)}, u32[]{:S(2)}, u32[]{:S(2)}) collective-permute-start(bf16[256,1024]{1,0:T(8,128)(2,1)S(1)} %bitcast_select_fusion.2), channel_id=1, source_target_pairs={{0,16},{16,0},{1,17},{17,1},{2,18},{18,2},{3,19},{19,3},{4,20},{20... | collective-permute-start | bytes 1572872 | tf_op jit(solution)/shard_map/ppermute | solution.py:11
  275.3 5.8 %copy-start.1 = (bf16[256,1024]{1,0:T(8,128)(2,1)S(1)}, bf16[256,1024]{1,0:T(8,128)(2,1)}, u32[]{:S(2)}) copy-start(bf16[256,1024]{1,0:T(8,128)(2,1)} %param.8) | copy-start | bytes 1572868

commit v2 on v1

--- a/solution.py
+++ b/solution.py
@@ -2,6 +2,7 @@
 import jax.numpy as jnp
 from jax import lax
 from jax.sharding import Mesh, PartitionSpec as P
+
 
 BF = jnp.bfloat16
 F32 = jnp.float32
@@ -52,7 +53,8 @@
     came = flip(send, "b")
     final_side = jnp.where(paired, 1 - half, half)
     keep, send = pick_two(side == final_side, mine, came)
-    return keep.astype(F32) + flip(send, "h").astype(F32)
+    came = flip(send, "h")
+    return keep.astype(F32) + came.astype(F32)
 
 
 def dot(a, b, a_dim, b_dim, kind=F32):
@@ -93,29 +95,32 @@
 
     def exchange(rows):
         return lax.all_to_all(
-            rows.reshape(experts, slot_cap, width),
+            rows.reshape(experts, slot_cap, rows.shape[1]),
             ("b", "l"),
             split_axis=0,
             concat_axis=0,
             tiled=True,
-        ).reshape(total_slots, width)
+        ).reshape(total_slots, rows.shape[1])
 
     send_x = dot(picks, tokens, 0, 0, BF)
     send_c = (slot_gate[:, None] * dot(picks, out_grad, 0, 0)).astype(BF)
-    recv_x = exchange(send_x)
-    recv_c = exchange(send_c)
+    both = exchange(jnp.concatenate([send_x, send_c], axis=1))
+    recv_x, recv_c = both[:, :width], both[:, width:]
 
     pre_gate = dot(recv_x, full_gate, 1, 0)
     pre_up = dot(recv_x, full_up, 1, 0)
     hidden = (jax.nn.silu(pre_gate) * pre_up).astype(BF)
+    pre_gate, pre_up, hidden = lax.optimization_barrier((pre_gate, pre_up, hidden))
     dw_down = dot(hidden, recv_c, 0, 0).astype(BF)
     grad_down = reduce_grad(dw_down, half, side, rest, paired)
     grad_h = dot(recv_c, full_down, 1, 1)
     sigmoid_a = jax.nn.sigmoid(pre_gate)
     grad_a = (grad_h * pre_up * sigmoid_a * (1.0 + pre_gate * (1.0 - sigmoid_a))).astype(BF)
     grad_b = (grad_h * pre_gate * sigmoid_a).astype(BF)
-    grad_gate = reduce_grad(dot(recv_x, grad_a, 0, 0).astype(BF), half, side, rest, paired)
-    grad_up = reduce_grad(dot(recv_x, grad_b, 0, 0).astype(BF), half, side, rest, paired)
+    dw_gate = dot(recv_x, grad_a, 0, 0).astype(BF)
+    grad_gate = reduce_grad(dw_gate, half, side, rest, paired)
+    dw_up = dot(recv_x, grad_b, 0, 0).astype(BF)
+    grad_up = reduce_grad(dw_up, half, side, rest, paired)
 
     expert_out = dot(hidden, full_down, 1, 0).astype(BF)
     returned_out = exchange(expert_out)

time: 282 us -> 281 us (level)
  starting transfers between devices: 57.4 us -> 45.7 us
  waiting for transfers between devices: 147 us -> 155 us
    ppermute x6, starting transfers between devices: 32.3 us -> 5.76 us  [flip_bit(): return lax.ppermute(value, axis, [(i, i ^ 1 << bit) for i in range(size)])]
    all_to_all x4 -> x3, starting transfers between devices: 18.7 us -> 27.5 us  [exchange(): lax.all_to_all(rows.reshape(experts, slot_cap, rows.shape[1]), ('b', 'l')...]
    ppermute x12, waiting for transfers between devices: 147 us -> 155 us  [flip(): return lax.ppermute(value, axis, [(0, 1), (1, 0)])]
    ppermute x12, starting transfers between devices: 6.32 us -> 12.4 us  [flip(): return lax.ppermute(value, axis, [(0, 1), (1, 0)])]
    select_n x14 -> x15, other arithmetic: 8.31 us -> 7.6 us  [pick_two(): return (jnp.where(first, low, high), jnp.where(first, high, low))]
  transfers between devices with their start and end apart: 22 -> 21, of which waited for: 9 -> 10; matrix products, arithmetic and copies ran while one was open for 19% -> 18% of each run, Pallas kernels for 0% -> 0%
where the time goes in v2:
time: 281 us; the launch traced here: 278 us
  waiting for transfers between devices  155 us (55%)
  starting transfers between devices  45.7 us (16%)
  matrix products  43.9 us (16%)
  other arithmetic  25.2 us (9%)
  local copies, waits for them, and re-layouts  6.08 us (2%)
    ppermute x12, waiting for transfers between devices, flip(): return lax.ppermute(value, axis, [(0, 1), (1, 0)])  155 us
    dot_general x15, matrix products, dot(): lax.dot_general(a, b, (((a_dim,), (b_dim,)), ((), ())), preferred_element...  43.9 us
    all_to_all x3, starting transfers between devices, exchange(): lax.all_to_all(rows.reshape(experts, slot_cap, rows.shape[1]), ('b', 'l')...  27.5 us
    ppermute x12, starting transfers between devices, flip(): return lax.ppermute(value, axis, [(0, 1), (1, 0)])  12.4 us
    select_n x15, other arithmetic, pick_two(): return (jnp.where(first, low, high), jnp.where(first, high, low))  7.6 us
    ppermute x6, starting transfers between devices, flip_bit(): return lax.ppermute(value, axis, [(i, i ^ 1 << bit) for i in range(size)])  5.76 us
  transfers between devices with their start and end apart: 21, of which 10 were waited for; matrix products, arithmetic and copies ran while one was open for 18% of the time, Pallas kernels for 0%

profile of v2, /device:TPU:31, one launch (start us, length us, event | category | flops | bytes accessed | tf_op | source)
XLA Modules:
  0.0 278.5 jit_solution(17327837835254184949)
XLA Ops:
  0.7 0.8 fusion.41
  1.5 0.8 fusion.42
  2.5 0.8 multiply_add_fusion
  3.3 0.8 fusion.16
  4.3 0.8 multiply_convert_fusion.3
  5.1 2.0 pad_maximum_fusion
  7.1 4.7 %all-to-all-start = ((bf16[8,96,2048]{2,1,0:T(8,128)(2,1)}), bf16[8,96,2048]{2,1,0:T(8,128)(2,1)}, u32[]{:S(2)}, u32[]{:S(2)}) async-start(bf16[8,96,2048]{2,1,0:T(8,128)(2,1)} %bitcast.8), calls=%async_computation | async-start | bytes 6291456 | tf_op jit(solution)/shard_map/all_to_all | solution.py:97
  11.8 2.3 collective-permute-start.6
  14.2 51.2 %collective-permute-done.3 = bf16[256,1024]{1,0:T(8,128)(2,1)S(1)} collective-permute-done((bf16[256,1024]{1,0:T(8,128)(2,1)S(1)}, bf16[256,1024]{1,0:T(8,128)(2,1)S(1)}, u32[]{:S(2)}, u32[]{:S(2)}) %collective-permute-start.3) | collective-permute-done | bytes 524320 | tf_op jit(solution)/shard_map/ppermute | solution.py:12
  65.5 0.3 collective-permute-start.4
  65.8 10.8 %collective-permute-done.6 = bf16[256,1024]{1,0:T(8,128)(2,1)S(1)} collective-permute-done((bf16[256,1024]{1,0:T(8,128)(2,1)S(1)}, bf16[256,1024]{1,0:T(8,128)(2,1)S(1)}, u32[]{:S(2)}, u32[]{:S(2)}) %collective-permute-start.6) | collective-permute-done | bytes 524320 | tf_op jit(solution)/shard_map/ppermute | solution.py:12
  77.1 10.8 %collective-permute-done = bf16[256,1024]{1,0:T(8,128)(2,1)S(1)} collective-permute-done((bf16[256,1024]{1,0:T(8,128)(2,1)S(1)}, bf16[256,1024]{1,0:T(8,128)(2,1)S(1)}, u32[]{:S(2)}, u32[]{:S(2)}) %collective-permute-start) | collective-permute-done | bytes 524320 | tf_op jit(solution)/shard_map/ppermute | solution.py:12
  88.0 0.3 collective-permute-start.1
  88.3 0.4 copy-done.7
  88.8 1.1 maximum_bitcast_fusion.1
  89.9 1.8 collective-permute-start.5
  91.8 1.1 maximum_bitcast_fusion.2
  92.9 6.8 %collective-permute-done.1 = bf16[256,1024]{1,0:T(8,128)(2,1)S(1)} collective-permute-done((bf16[256,1024]{1,0:T(8,128)(2,1)S(1)}, bf16[256,1024]{1,0:T(8,128)(2,1)S(1)}, u32[]{:S(2)}, u32[]{:S(2)}) %collective-permute-start.1) | collective-permute-done | bytes 524320 | tf_op jit(solution)/shard_map/ppermute | solution.py:12
  99.8 1.1 maximum_bitcast_fusion
  100.9 2.7 collective-permute-start.2
  103.5 0.6 fusion.43
  105.4 1.4 bitcast_select_fusion.1
  107.0 1.6 copy.22
  108.5 1.4 broadcast_select_fusion.3
  109.9 1.5 pad_maximum_fusion.3
  111.4 1.4 broadcast_select_fusion.6
  112.8 1.5 pad_maximum_fusion.1
  114.3 4.0 %fusion.9 = f32[768,1024]{1,0:T(8,128)S(1)} fusion(bf16[1024,1024]{1,0:T(8,128)(2,1)} %bitcast.124, bf16[768,2048]{1,0:T(8,128)(2,1)} %bitcast.9), kind=kOutput, calls=%fused_computation.44 | convolution fusion | flops 1610612736 | bytes 6815744 | tf_op jit(solution)/shard_map/dot_general | solution.py:61
  118.4 6.2 %multiply_convert_fusion.2 = (bf16[768,1024]{1,0:T(8,128)(2,1)S(1)}, f32[768,1024]{1,0:T(8,128)}) fusion(f32[768,1024]{1,0:T(8,128)S(1)} %fusion.9, bf16[1024,1024]{1,0:T(8,128)(2,1)S(1)} %bitcast.122, bf16[768,2048]{1,0:T(8,128)(2,1)} %bitcast.9), kind=kOutput, calls=%fused_computation.5 | convolution fusion | flops 1615331328 | bytes 11534336 | tf_op jit(solution)/shard_map/dot_general | solution.py:61
  124.6 2.9 %convolution_convert_fusion.3 = bf16[768,1024]{1,0:T(8,128)(2,1)} fusion(bf16[768,1024]{1,0:T(8,128)(2,1)S(1)} %get-tuple-element.8, bf16[1024,1024]{1,0:T(8,128)(2,1)S(1)} %bitcast.127), kind=kOutput, calls=%fused_computation.18 | convolution fusion | flops 1611399168 | bytes 5242880 | tf_op jit(solution)/shard_map/dot_general | solution.py:61
  127.5 18.3 %all-to-all-start.1 = ((bf16[8,96,1024]{2,1,0:T(8,128)(2,1)}), bf16[8,96,1024]{2,1,0:T(8,128)(2,1)}, u32[]{:S(2)}, u32[]{:S(2)}) async-start(bf16[8,96,1024]{2,1,0:T(8,128)(2,1)} %bitcast.129), calls=%async_computation.1 | async-start | bytes 3145728 | tf_op jit(solution)/shard_map/all_to_all | solution.py:97
  145.8 6.6 %multiply_convert_fusion.1 = (bf16[768,1024]{1,0:T(8,128)(2,1)S(1)}, bf16[768,1024]{1,0:T(8,128)(2,1)S(1)}) fusion(f32[768,1024]{1,0:T(8,128)} %copy-done.15, f32[768,1024]{1,0:T(8,128)} %get-tuple-element.9, bf16[1024,1024]{1,0:T(8,128)(2,1)} %bitcast.126, bf16[768,2048]{1,0:T(8,128)(2,1)} %bitcast.9), kind=kOutput, calls=%fused_computation.3 | convolution fusion | flops 1620836352 | bytes 13107200 | tf_op jit(solution)/shard_map/dot_general | solution.py:61
  152.4 3.2 %convolution_convert_fusion.2 = bf16[1024,1024]{1,0:T(8,128)(2,1)S(1)} fusion(bf16[768,1024]{1,0:T(8,128)(2,1)S(1)} %get-tuple-element.35, bf16[768,2048]{1,0:T(8,128)(2,1)} %bitcast.9), kind=kOutput, calls=%fused_computation.17 | convolution fusion | flops 1611661312 | bytes 5242880 | tf_op jit(solution)/shard_map/dot_general | solution.py:61
  155.7 3.2 %convolution_convert_fusion.1 = bf16[1024,1024]{1,0:T(8,128)(2,1)S(1)} fusion(bf16[768,1024]{1,0:T(8,128)(2,1)S(1)} %get-tuple-element.36, bf16[768,2048]{1,0:T(8,128)(2,1)} %bitcast.9), kind=kOutput, calls=%fused_computation.16 | convolution fusion | flops 1611661312 | bytes 5242880 | tf_op jit(solution)/shard_map/dot_general | solution.py:61
  159.2 0.6 collective-permute-start.12
  159.9 0.6 copy-done.17
  160.4 3.2 %convolution_convert_fusion = bf16[1024,1024]{1,0:T(8,128)(2,1)S(1)} fusion(bf16[768,1024]{1,0:T(8,128)(2,1)S(1)} %copy-done.17, bf16[768,2048]{1,0:T(8,128)(2,1)} %bitcast.9), kind=kOutput, calls=%fused_computation.15 | convolution fusion | flops 1611661312 | bytes 5242880 | tf_op jit(solution)/shard_map/dot_general | solution.py:61
  163.7 1.3 copy-done.2
  165.1 1.1 broadcast_select_fusion.4
  166.1 0.6 collective-permute-start.15
  166.7 1.8 fusion.44
  168.5 3.0 %add_convert_fusion = bf16[768,1024]{1,0:T(8,128)(2,1)} fusion(f32[768,1024]{1,0:T(8,128)S(1)} %fusion.44, bf16[768,1024]{1,0:T(8,128)(2,1)S(1)} %get-tuple-element.35, bf16[1024,1024]{1,0:T(8,128)(2,1)S(1)} %bitcast.125), kind=kOutput, calls=%fused_computation.1 | convolution fusion | flops 1612185600 | bytes 8388608 | tf_op jit(solution)/shard_map/dot_general | solution.py:61
  171.5 0.6 add_convert_fusion.2
  172.2 0.9 select_bitcast_fusion.1
  173.3 0.8 add_convert_fusion.3
  174.1 0.9 select_bitcast_fusion.2
  175.0 1.2 collective-permute-start.10
  176.2 4.5 %all-to-all-start.2 = ((bf16[8,96,1024]{2,1,0:T(8,128)(2,1)}), bf16[8,96,1024]{2,1,0:T(8,128)(2,1)}, u32[]{:S(2)}, u32[]{:S(2)}) async-start(bf16[8,96,1024]{2,1,0:T(8,128)(2,1)} %bitcast.128), calls=%async_computation.2 | async-start | bytes 3145728 | tf_op jit(solution)/shard_map/all_to_all | solution.py:97
  180.7 2.5 add_convert_fusion.1
  183.6 15.8 %collective-permute-done.13 = bf16[256,1024]{1,0:T(8,128)(2,1)S(1)} collective-permute-done((bf16[256,1024]{1,0:T(8,128)(2,1)}, bf16[256,1024]{1,0:T(8,128)(2,1)S(1)}, u32[]{:S(2)}, u32[]{:S(2)}) %collective-permute-start.13) | collective-permute-done | bytes 524320 | tf_op jit(solution)/shard_map/ppermute | solution.py:12
  199.5 2.4 collective-permute-start.14
  201.9 8.7 %collective-permute-done.10 = bf16[256,1024]{1,0:T(8,128)(2,1)S(1)} collective-permute-done((bf16[256,1024]{1,0:T(8,128)(2,1)}, bf16[256,1024]{1,0:T(8,128)(2,1)S(1)}, u32[]{:S(2)}, u32[]{:S(2)}) %collective-permute-start.10) | collective-permute-done | bytes 524320 | tf_op jit(solution)/shard_map/ppermute | solution.py:12
  210.7 2.4 collective-permute-start.11
  213.0 13.0 %collective-permute-done.16 = bf16[256,1024]{1,0:T(8,128)(2,1)S(1)} collective-permute-done((bf16[256,1024]{1,0:T(8,128)(2,1)S(1)}, bf16[256,1024]{1,0:T(8,128)(2,1)S(1)}, u32[]{:S(2)}, u32[]{:S(2)}) %collective-permute-start.16) | collective-permute-done | bytes 524320 | tf_op jit(solution)/shard_map/ppermute | solution.py:12
  226.2 2.4 collective-permute-start.17
  228.5 18.4 %collective-permute-done.14 = bf16[256,1024]{1,0:T(8,128)(2,1)S(1)} collective-permute-done((bf16[256,1024]{1,0:T(8,128)(2,1)S(1)}, bf16[256,1024]{1,0:T(8,128)(2,1)S(1)}, u32[]{:S(2)}, u32[]{:S(2)}) %collective-permute-start.14) | collective-permute-done | bytes 524320 | tf_op jit(solution)/shard_map/ppermute | solution.py:12
  246.9 1.3 add_bitcast_fusion.1
  248.2 9.9 %collective-permute-done.11 = bf16[256,1024]{1,0:T(8,128)(2,1)S(1)} collective-permute-done((bf16[256,1024]{1,0:T(8,128)(2,1)S(1)}, bf16[256,1024]{1,0:T(8,128)(2,1)S(1)}, u32[]{:S(2)}, u32[]{:S(2)}) %collective-permute-start.11) | collective-permute-done | bytes 524320 | tf_op jit(solution)/shard_map/ppermute | solution.py:12
  258.1 1.3 add_bitcast_fusion.2
  259.4 9.9 %collective-permute-done.17 = bf16[256,1024]{1,0:T(8,128)(2,1)S(1)} collective-permute-done((bf16[256,1024]{1,0:T(8,128)(2,1)S(1)}, bf16[256,1024]{1,0:T(8,128)(2,1)S(1)}, u32[]{:S(2)}, u32[]{:S(2)}) %collective-permute-start.17) | collective-permute-done | bytes 524320 | tf_op jit(solution)/shard_map/ppermute | solution.py:12
  269.4 1.3 add_bitcast_fusion
  270.7 2.0 convolution_multiply_fusion.1
  272.7 2.9 %fusion.4 = bf16[256,1024]{1,0:T(8,128)(2,1)} fusion(f32[256,1024]{1,0:T(8,128)S(1)} %convolution_multiply_fusion.1, bf16[768,1024]{1,0:T(8,128)(2,1)} %bitcast.28, f32[256]{0:T(256)S(1)} %bitcast.131, s32[256]{0:T(256)S(1)} %bitcast.137), kind=kOutput, calls=%fused_computation.25 | convolution fusion | flops 403636224 | bytes 3147776 | tf_op jit(solution)/shard_map/dot_general | solution.py:61
  275.6 2.9 %convolution_convert_fusion.4 = bf16[256,1024]{1,0:T(8,128)(2,1)} fusion(bf16[768,1024]{1,0:T(8,128)(2,1)} %bitcast.30, s32[256]{0:T(256)S(1)} %bitcast.138, s32[256]{0:T(256)S(1)} %bitcast.143), kind=kOutput, calls=%fused_computation.26 | convolution fusion | flops 404488192 | bytes 2099200 | tf_op jit(solution)/shard_map/dot_general | solution.py:61
  (70 shorter events, 3.0 us)
Async XLA Ops:
  0.6 2.6 copy-start
  0.6 3.6 %copy-start.14 = (bf16[256,1024]{1,0:T(8,128)(2,1)S(1)}, bf16[256,1024]{1,0:T(8,128)(2,1)}, u32[]{:S(2)}) copy-start(bf16[256,1024]{1,0:T(8,128)(2,1)} %param.15) | copy-start | bytes 1572868
  7.1 4.7 %copy-start.3 = (bf16[1,256,1024]{2,1,0:T(8,128)(2,1)S(1)}, bf16[1,256,1024]{2,1,0:T(8,128)(2,1)}, u32[]{:S(2)}) copy-start(bf16[1,256,1024]{2,1,0:T(8,128)(2,1)} %param.12) | copy-start | bytes 1572868
  7.1 4.7 %copy-start.4 = (bf16[1,256,1024]{2,1,0:T(8,128)(2,1)S(1)}, bf16[1,256,1024]{2,1,0:T(8,128)(2,1)}, u32[]{:S(2)}) copy-start(bf16[1,256,1024]{2,1,0:T(8,128)(2,1)} %param.13) | copy-start | bytes 1572868
  7.1 7.0 %copy-start.5 = (bf16[1,256,1024]{2,1,0:T(8,128)(2,1)S(1)}, bf16[1,256,1024]{2,1,0:T(8,128)(2,1)}, u32[]{:S(2)}) copy-start(bf16[1,256,1024]{2,1,0:T(8,128)(2,1)} %param.11) | copy-start | bytes 1572868
  7.1 107.2 %all-to-all-start = ((bf16[8,96,2048]{2,1,0:T(8,128)(2,1)}), bf16[8,96,2048]{2,1,0:T(8,128)(2,1)}, u32[]{:S(2)}, u32[]{:S(2)}) async-start(bf16[8,96,2048]{2,1,0:T(8,128)(2,1)} %bitcast.8), calls=%async_computation | async-start | bytes 6291456 | tf_op jit(solution)/shard_map/all_to_all | solution.py:97
  11.8 53.7 %collective-permute-start.3 = (bf16[256,1024]{1,0:T(8,128)(2,1)S(1)}, bf16[256,1024]{1,0:T(8,128)(2,1)S(1)}, u32[]{:S(2)}, u32[]{:S(2)}) collective-permute-start(bf16[256,1024]{1,0:T(8,128)(2,1)S(1)} %bitcast.119), channel_id=1, source_target_pairs={{0,16},{16,0},{1,17},{17,1},{2,18},{18,2},{3,19},{19,3},{4,20},{20... | collective-permute-start | bytes 1572872 | tf_op jit(solution)/shard_map/ppermute | solution.py:12
  11.8 64.8 %collective-permute-start.6 = (bf16[256,1024]{1,0:T(8,128)(2,1)S(1)}, bf16[256,1024]{1,0:T(8,128)(2,1)S(1)}, u32[]{:S(2)}, u32[]{:S(2)}) collective-permute-start(bf16[256,1024]{1,0:T(8,128)(2,1)S(1)} %bitcast.120), channel_id=1, source_target_pairs={{0,16},{16,0},{1,17},{17,1},{2,18},{18,2},{3,19},{19,3},{4,20},{20... | collective-permute-start | bytes 1572872 | tf_op jit(solution)/shard_map/ppermute | solution.py:12
  14.1 73.8 %collective-permute-start = (bf16[256,1024]{1,0:T(8,128)(2,1)S(1)}, bf16[256,1024]{1,0:T(8,128)(2,1)S(1)}, u32[]{:S(2)}, u32[]{:S(2)}) collective-permute-start(bf16[256,1024]{1,0:T(8,128)(2,1)S(1)} %bitcast.121), channel_id=1, source_target_pairs={{0,16},{16,0},{1,17},{17,1},{2,18},{18,2},{3,19},{19,3},{4,20},{20... | collective-permute-start | bytes 1572872 | tf_op jit(solution)/shard_map/ppermute | solution.py:12
  65.4 22.5 %copy-start.9 = (bf16[256,1024]{1,0:T(8,128)(2,1)}, bf16[256,1024]{1,0:T(8,128)(2,1)S(1)}, u32[]{:S(2)}) copy-start(bf16[256,1024]{1,0:T(8,128)(2,1)S(1)} %collective-permute-done.3) | copy-start | bytes 1572868
  65.5 23.2 %collective-permute-start.4 = (bf16[256,1024]{1,0:T(8,128)(2,1)S(1)}, bf16[256,1024]{1,0:T(8,128)(2,1)S(1)}, u32[]{:S(2)}, u32[]{:S(2)}) collective-permute-start(bf16[256,1024]{1,0:T(8,128)(2,1)S(1)} %broadcast_select_fusion.12), channel_id=1, source_target_pairs={{0,2},{2,0},{1,3},{3,1},{4,6},{6,4},{5,7},{7,5},{8,10},{10,8},{9,1... | collective-permute-start | bytes 1572872 | tf_op jit(solution)/shard_map/ppermute | solution.py:12
  76.7 15.0 %collective-permute-start.7 = (bf16[256,1024]{1,0:T(8,128)(2,1)S(1)}, bf16[256,1024]{1,0:T(8,128)(2,1)S(1)}, u32[]{:S(2)}, u32[]{:S(2)}) collective-permute-start(bf16[256,1024]{1,0:T(8,128)(2,1)S(1)} %broadcast_select_fusion.10), channel_id=1, source_target_pairs={{0,2},{2,0},{1,3},{3,1},{4,6},{6,4},{5,7},{7,5},{8,10},{10,8},{9,1... | collective-permute-start | bytes 1572872 | tf_op jit(solution)/shard_map/ppermute | solution.py:12
  87.9 0.8 copy-start.7
  88.0 11.7 %collective-permute-start.1 = (bf16[256,1024]{1,0:T(8,128)(2,1)S(1)}, bf16[256,1024]{1,0:T(8,128)(2,1)S(1)}, u32[]{:S(2)}, u32[]{:S(2)}) collective-permute-start(bf16[256,1024]{1,0:T(8,128)(2,1)S(1)} %broadcast_select_fusion.14), channel_id=1, source_target_pairs={{0,2},{2,0},{1,3},{3,1},{4,6},{6,4},{5,7},{7,5},{8,10},{10,8},{9,1... | collective-permute-start | bytes 1572872 | tf_op jit(solution)/shard_map/ppermute | solution.py:12
  89.9 9.8 %copy-start.6 = (bf16[1,256,1024]{2,1,0:T(8,128)(2,1)S(1)}, bf16[1,256,1024]{2,1,0:T(8,128)(2,1)}, u32[]{:S(2)}) copy-start(bf16[1,256,1024]{2,1,0:T(8,128)(2,1)} %param.11) | copy-start | bytes 1572868
  89.9 9.8 %copy-start.8 = (bf16[256,1024]{1,0:T(8,128)(2,1)S(1)}, bf16[256,1024]{1,0:T(8,128)(2,1)}, u32[]{:S(2)}) copy-start(bf16[256,1024]{1,0:T(8,128)(2,1)} %copy-done.7) | copy-start | bytes 1572868
  89.9 15.5 %collective-permute-start.5 = (bf16[2,1,256,1024]{3,2,0,1:T(8,128)(2,1)}, bf16[2,1,256,1024]{3,2,0,1:T(8,128)(2,1)}, u32[]{:S(2)}, u32[]{:S(2)}) collective-permute-start(bf16[2,1,256,1024]{3,2,0,1:T(8,128)(2,1)} %maximum_bitcast_fusion.1), channel_id=1, source_target_pairs={{0,1},{1,0},{2,3},{3,2},{4,5},{5,4},{6,7},{7,6},{8,9},{9,8},{10,11... | collective-permute-start | bytes 3145736 | tf_op jit(solution)/shard_map/ppermute | solution.py:17
  92.8 10.7 %copy-start.13 = (s32[8]{0:T(128)S(1)}, s32[8]{0:T(128)}, u32[]{:S(2)}) copy-start(s32[8]{0:T(128)} %param.14) | copy-start | bytes 100
  92.8 15.7 %collective-permute-start.8 = (bf16[2,1,256,1024]{3,2,1,0:T(8,128)(2,1)}, bf16[2,1,256,1024]{3,2,1,0:T(8,128)(2,1)}, u32[]{:S(2)}, u32[]{:S(2)}) collective-permute-start(bf16[2,1,256,1024]{3,2,1,0:T(8,128)(2,1)} %maximum_bitcast_fusion.2), channel_id=1, source_target_pairs={{0,1},{1,0},{2,3},{3,2},{4,5},{5,4},{6,7},{7,6},{8,9},{9,8},{10,11... | collective-permute-start | bytes 3145736 | tf_op jit(solution)/shard_map/ppermute | solution.py:17
  100.9 10.6 %collective-permute-start.2 = (bf16[2,1,256,1024]{3,2,1,0:T(8,128)(2,1)}, bf16[2,1,256,1024]{3,2,1,0:T(8,128)(2,1)}, u32[]{:S(2)}, u32[]{:S(2)}) collective-permute-start(bf16[2,1,256,1024]{3,2,1,0:T(8,128)(2,1)} %maximum_bitcast_fusion), channel_id=1, source_target_pairs={{0,1},{1,0},{2,3},{3,2},{4,5},{5,4},{6,7},{7,6},{8,9},{9,8},{10,11... | collective-permute-start | bytes 3145736 | tf_op jit(solution)/shard_map/ppermute | solution.py:17
  114.3 4.0 %copy-start.10 = (bf16[2,2,256,1024]{3,2,1,0:T(8,128)(2,1)S(1)}, bf16[2,2,256,1024]{3,2,1,0:T(8,128)(2,1)}, u32[]{:S(2)}) copy-start(bf16[2,2,256,1024]{3,2,1,0:T(8,128)(2,1)} %copy.22) | copy-start | bytes 6291460
  118.3 6.3 %copy-start.15 = (f32[768,1024]{1,0:T(8,128)}, f32[768,1024]{1,0:T(8,128)S(1)}, u32[]{:S(2)}) copy-start(f32[768,1024]{1,0:T(8,128)S(1)} %fusion.9) | copy-start | bytes 9437188
  118.3 6.3 %copy-start.12 = (bf16[2,2,256,1024]{3,2,1,0:T(8,128)(2,1)S(1)}, bf16[2,2,256,1024]{3,2,1,0:T(8,128)(2,1)}, u32[]{:S(2)}) copy-start(bf16[2,2,256,1024]{3,2,1,0:T(8,128)(2,1)} %pad_maximum_fusion.3) | copy-start | bytes 6291460
  124.6 2.9 %copy-start.16 = (bf16[768,1024]{1,0:T(8,128)(2,1)}, bf16[768,1024]{1,0:T(8,128)(2,1)S(1)}, u32[]{:S(2)}) copy-start(bf16[768,1024]{1,0:T(8,128)(2,1)S(1)} %get-tuple-element.8) | copy-start | bytes 4718596
  127.5 48.6 %all-to-all-start.1 = ((bf16[8,96,1024]{2,1,0:T(8,128)(2,1)}), bf16[8,96,1024]{2,1,0:T(8,128)(2,1)}, u32[]{:S(2)}, u32[]{:S(2)}) async-start(bf16[8,96,1024]{2,1,0:T(8,128)(2,1)} %bitcast.129), calls=%async_computation.1 | async-start | bytes 3145728 | tf_op jit(solution)/shard_map/all_to_all | solution.py:97
  159.0 1.4 copy-start.17
  159.2 12.4 %collective-permute-start.12 = (bf16[2,1,256,1024]{3,2,1,0:T(8,128)(2,1)S(1)}, bf16[2,1,256,1024]{3,2,1,0:T(8,128)(2,1)S(1)}, u32[]{:S(2)}, u32[]{:S(2)}) collective-permute-start(bf16[2,1,256,1024]{3,2,1,0:T(8,128)(2,1)S(1)} %broadcast_select_fusion), channel_id=1, source_target_pairs={{0,1},{1,0},{2,3},{3,2},{4,5},{5,4},{6,7},{7,6},{8,9},{9,8},{10,11... | collective-permute-start | bytes 3145736 | tf_op jit(solution)/shard_map/ppermute | solution.py:17
  159.8 13.5 %collective-permute-start.9 = (bf16[2,1,256,1024]{3,2,1,0:T(8,128)(2,1)S(1)}, bf16[2,1,256,1024]{3,2,1,0:T(8,128)(2,1)S(1)}, u32[]{:S(2)}, u32[]{:S(2)}) collective-permute-start(bf16[2,1,256,1024]{3,2,1,0:T(8,128)(2,1)S(1)} %broadcast_select_fusion.1), channel_id=1, source_target_pairs={{0,1},{1,0},{2,3},{3,2},{4,5},{5,4},{6,7},{7,6},{8,9},{9,8},{10,11... | collective-permute-start | bytes 3145736 | tf_op jit(solution)/shard_map/ppermute | solution.py:17
  163.7 1.4 copy-start.2
  166.1 2.4 copy-start.11
  166.1 14.6 %collective-permute-start.15 = (bf16[2,1,256,1024]{3,2,1,0:T(8,128)(2,1)}, bf16[2,1,256,1024]{3,2,1,0:T(8,128)(2,1)}, u32[]{:S(2)}, u32[]{:S(2)}) collective-permute-start(bf16[2,1,256,1024]{3,2,1,0:T(8,128)(2,1)} %broadcast_select_fusion.4), channel_id=1, source_target_pairs={{0,1},{1,0},{2,3},{3,2},{4,5},{5,4},{6,7},{7,6},{8,9},{9,8},{10,11... | collective-permute-start | bytes 3145736 | tf_op jit(solution)/shard_map/ppermute | solution.py:17
  173.0 26.4 %collective-permute-start.13 = (bf16[256,1024]{1,0:T(8,128)(2,1)}, bf16[256,1024]{1,0:T(8,128)(2,1)S(1)}, u32[]{:S(2)}, u32[]{:S(2)}) collective-permute-start(bf16[256,1024]{1,0:T(8,128)(2,1)} %select_bitcast_fusion.1), channel_id=1, source_target_pairs={{0,2},{2,0},{1,3},{3,1},{4,6},{6,4},{5,7},{7,5},{8,10},{10,8},{9,1... | collective-permute-start | bytes 1572872 | tf_op jit(solution)/shard_map/ppermute | solution.py:12
  175.0 35.6 %collective-permute-start.10 = (bf16[256,1024]{1,0:T(8,128)(2,1)}, bf16[256,1024]{1,0:T(8,128)(2,1)S(1)}, u32[]{:S(2)}, u32[]{:S(2)}) collective-permute-start(bf16[256,1024]{1,0:T(8,128)(2,1)} %select_bitcast_fusion.2), channel_id=1, source_target_pairs={{0,2},{2,0},{1,3},{3,1},{4,6},{6,4},{5,7},{7,5},{8,10},{10,8},{9,1... | collective-permute-start | bytes 1572872 | tf_op jit(solution)/shard_map/ppermute | solution.py:12
  176.2 99.4 %all-to-all-start.2 = ((bf16[8,96,1024]{2,1,0:T(8,128)(2,1)}), bf16[8,96,1024]{2,1,0:T(8,128)(2,1)}, u32[]{:S(2)}, u32[]{:S(2)}) async-start(bf16[8,96,1024]{2,1,0:T(8,128)(2,1)} %bitcast.128), calls=%async_computation.2 | async-start | bytes 3145728 | tf_op jit(solution)/shard_map/all_to_all | solution.py:97
  183.3 42.7 %collective-permute-start.16 = (bf16[256,1024]{1,0:T(8,128)(2,1)S(1)}, bf16[256,1024]{1,0:T(8,128)(2,1)S(1)}, u32[]{:S(2)}, u32[]{:S(2)}) collective-permute-start(bf16[256,1024]{1,0:T(8,128)(2,1)S(1)} %select_bitcast_fusion), channel_id=1, source_target_pairs={{0,2},{2,0},{1,3},{3,1},{4,6},{6,4},{5,7},{7,5},{8,10},{10,8},{9,1... | collective-permute-start | bytes 1572872 | tf_op jit(solution)/shard_map/ppermute | solution.py:12
  199.5 47.4 %collective-permute-start.14 = (bf16[256,1024]{1,0:T(8,128)(2,1)S(1)}, bf16[256,1024]{1,0:T(8,128)(2,1)S(1)}, u32[]{:S(2)}, u32[]{:S(2)}) collective-permute-start(bf16[256,1024]{1,0:T(8,128)(2,1)S(1)} %bitcast_select_fusion.4), channel_id=1, source_target_pairs={{0,16},{16,0},{1,17},{17,1},{2,18},{18,2},{3,19},{19,3},{4,20},{20... | collective-permute-start | bytes 1572872 | tf_op jit(solution)/shard_map/ppermute | solution.py:12
  210.7 47.5 %collective-permute-start.11 = (bf16[256,1024]{1,0:T(8,128)(2,1)S(1)}, bf16[256,1024]{1,0:T(8,128)(2,1)S(1)}, u32[]{:S(2)}, u32[]{:S(2)}) collective-permute-start(bf16[256,1024]{1,0:T(8,128)(2,1)S(1)} %bitcast_select_fusion.6), channel_id=1, source_target_pairs={{0,16},{16,0},{1,17},{17,1},{2,18},{18,2},{3,19},{19,3},{4,20},{20... | collective-permute-start | bytes 1572872 | tf_op jit(solution)/shard_map/ppermute | solution.py:12
  226.2 43.2 %collective-permute-start.17 = (bf16[256,1024]{1,0:T(8,128)(2,1)S(1)}, bf16[256,1024]{1,0:T(8,128)(2,1)S(1)}, u32[]{:S(2)}, u32[]{:S(2)}) collective-permute-start(bf16[256,1024]{1,0:T(8,128)(2,1)S(1)} %bitcast_select_fusion.2), channel_id=1, source_target_pairs={{0,16},{16,0},{1,17},{17,1},{2,18},{18,2},{3,19},{19,3},{4,20},{20... | collective-permute-start | bytes 1572872 | tf_op jit(solution)/shard_map/ppermute | solution.py:12
  272.7 5.8 %copy-start.1 = (bf16[256,1024]{1,0:T(8,128)(2,1)S(1)}, bf16[256,1024]{1,0:T(8,128)(2,1)}, u32[]{:S(2)}) copy-start(bf16[256,1024]{1,0:T(8,128)(2,1)} %param.8) | copy-start | bytes 1572868
